TPU v7x, 32 devices: a whole 2x2x4 slice. The times are simulated.
32 devices in a mesh: dap: 8 (over y, x, core), seq: 4 (over z).
Axes of the slice: x: 2, y: 2, z: 4, core: 2. Of those that a mesh axis runs over, the one named last changes fastest.
Arguments:
- homolog_tensor: bfloat16 [8, 32, 256], P('dap', 'seq'), may hold values from -6 to 6
- pair_features: bfloat16 [32, 32, 128], P('seq', 'dap'), may hold values from -6 to 6
- entry_real_mask: int32 [8, 32], P('dap', 'seq'), may hold values 0 or 1
- chain_ids: int32 [32], replicated, may hold values from 0 to 3, never falling along the last dimension, each value on 1 to 16 neighbouring positions
- horizontal_matrices: bfloat16 [256, 1024], replicated, may hold values from -0.375 to 0.375
- horizontal_projector: bfloat16 [256, 256], replicated, may hold values from -0.375 to 0.375
- bias_proj: float32 [128, 8], replicated, may hold values from -35.35534 to 35.35534
- chain_bias: float32 [2, 8], replicated, may hold values from -4 to 4
- column_proj: bfloat16 [256, 1024], replicated, may hold values from -12.5 to 12.5
- vertical_projector: bfloat16 [256, 256], replicated, may hold values from -0.375 to 0.375
- expansion_matrix: bfloat16 [256, 1024], replicated, may hold values from -0.375 to 0.375
- contraction_matrix: bfloat16 [1024, 256], replicated, may hold values from -0.1875 to 0.1875
Outputs:
- updated: bfloat16 [8, 32, 256], P('dap', 'seq')
Inputs may be any that keep to these rules, and one draw needn't show every extreme that they name: `chain_ids`: chain numbers never fall along the residues.
All inputs are finite; a program needn't handle non-finite values. No bound on the sum of `entry_real_mask` on one device may be relied on, other than what follows from the above.
Results may differ from a plain program's by a relative error of at most 0.013.
The roundings to bfloat16 on the way count: a program that leaves them out, or rounds other values in their place, can miss the bound.
Values may be sent and summed in bfloat16 or wider, within the bound.
No kernel may reach another device: no remote copies, remote signals or barrier semaphores. Data moves between devices by JAX's collectives and lax.ppermute only.
A program may use at most 64 MiB of HBM per device.

v0:
```python
import jax
import jax.numpy as jnp
from jax import lax
from jax.sharding import PartitionSpec as P

HEAD_TOTAL = 8
HEAD_DEPTH = 32


epsilon = 1e-05


def layer_norm(inputs):
    center = inputs - jnp.mean(inputs, axis=-1, keepdims=True)
    spread = jnp.mean(center * center, axis=-1, keepdims=True)
    return center * lax.rsqrt(spread + epsilon)


def attend(queries, key_part, value_part, keep_mask, bias_term):
    scores = jnp.einsum(
        "ihd,jhd->hij", queries, key_part, preferred_element_type=jnp.float32
    ) * HEAD_DEPTH ** (-0.5)
    if bias_term is not None:
        scores = scores + bias_term.astype(jnp.float32)
    scores = jnp.where(keep_mask[None, None, :] > 0, scores, -1000000000.0)
    weights = jax.nn.softmax(scores, axis=-1).astype(jnp.bfloat16)
    return jnp.einsum("hij,jhd->ihd", weights, value_part, preferred_element_type=jnp.float32)


def column_update(
    column, keep_column, column_proj, vertical_projector, expansion_matrix, contraction_matrix
):
    expanded_dimension = HEAD_TOTAL * HEAD_DEPTH
    standardized = layer_norm(column.astype(jnp.float32)).astype(jnp.bfloat16)
    projected = jnp.dot(standardized, column_proj, preferred_element_type=jnp.float32).astype(
        jnp.bfloat16
    )
    queries = projected[:, :expanded_dimension].reshape(-1, HEAD_TOTAL, HEAD_DEPTH)
    key_part = projected[:, expanded_dimension : 2 * expanded_dimension].reshape(
        -1, HEAD_TOTAL, HEAD_DEPTH
    )
    value_part = projected[:, 2 * expanded_dimension : 3 * expanded_dimension].reshape(
        -1, HEAD_TOTAL, HEAD_DEPTH
    )
    attended = attend(queries, key_part, value_part, keep_column, None).reshape(
        -1, expanded_dimension
    )
    sigmoid_scaled = (
        jax.nn.sigmoid(projected[:, 3 * expanded_dimension :].astype(jnp.float32)) * attended
    ).astype(jnp.bfloat16)
    mixed = column.astype(jnp.float32) + jnp.dot(
        sigmoid_scaled, vertical_projector, preferred_element_type=jnp.float32
    )
    inner = jnp.maximum(
        jnp.dot(
            layer_norm(mixed).astype(jnp.bfloat16),
            expansion_matrix,
            preferred_element_type=jnp.float32,
        ),
        0.0,
    ).astype(jnp.bfloat16)
    return (mixed + jnp.dot(inner, contraction_matrix, preferred_element_type=jnp.float32)).astype(
        jnp.bfloat16
    )


def body(
    homolog_tensor,
    pair_features,
    entry_real_mask,
    chain_ids,
    horizontal_matrices,
    horizontal_projector,
    bias_proj,
    chain_bias,
    column_proj,
    vertical_projector,
    expansion_matrix,
    contraction_matrix,
):
    row_count, local_residues, channels = homolog_tensor.shape
    expanded_dimension = HEAD_TOTAL * HEAD_DEPTH
    dap_count = lax.axis_size("dap")
    pair_rows, pair_columns, pair_width = pair_features.shape
    normed_pair = layer_norm(pair_features.astype(jnp.float32))
    projected_pair = jnp.einsum(
        "ijc,ch->hij", normed_pair, bias_proj, precision=lax.Precision.HIGHEST
    )
    row_chain = lax.dynamic_slice_in_dim(chain_ids, lax.axis_index("seq") * pair_rows, pair_rows)
    column_chain = lax.dynamic_slice_in_dim(
        chain_ids, lax.axis_index("dap") * pair_columns, pair_columns
    )
    same_chain = (row_chain[:, None] == column_chain[None, :]).astype(jnp.float32)
    chain_term = chain_bias[0][:, None, None] * same_chain + chain_bias[1][:, None, None] * (
        1.0 - same_chain
    )
    local_bias = (projected_pair + chain_term).astype(jnp.bfloat16)
    pair_bias = lax.all_gather(local_bias, "dap", axis=2, tiled=True)
    standardized = layer_norm(homolog_tensor.astype(jnp.float32)).astype(jnp.bfloat16)
    flat = standardized.reshape(-1, channels)
    keep_mask = entry_real_mask.astype(jnp.bfloat16)
    projected = (
        jnp.dot(flat, horizontal_matrices, preferred_element_type=jnp.float32)
        .astype(jnp.bfloat16)
        .reshape(row_count, local_residues, 4 * expanded_dimension)
    )
    queries = projected[..., :expanded_dimension]
    gating = projected[..., 3 * expanded_dimension :]
    key_values, keep_all = (
        lax.all_gather(
            projected[..., expanded_dimension : 3 * expanded_dimension], "seq", axis=1, tiled=True
        ),
        lax.all_gather(keep_mask, "seq", axis=1, tiled=True),
    )

    def one_row(inputs_row):
        row_queries, row_pairs, row_keep = inputs_row
        key_part = row_pairs[:, :expanded_dimension].reshape(-1, HEAD_TOTAL, HEAD_DEPTH)
        value_part = row_pairs[:, expanded_dimension:].reshape(-1, HEAD_TOTAL, HEAD_DEPTH)
        return attend(
            row_queries.reshape(local_residues, HEAD_TOTAL, HEAD_DEPTH),
            key_part,
            value_part,
            row_keep,
            pair_bias,
        ).reshape(local_residues, expanded_dimension)

    attended = lax.map(one_row, (queries, key_values, keep_all))
    sigmoid_scaled = (jax.nn.sigmoid(gating.astype(jnp.float32)) * attended).astype(jnp.bfloat16)
    row_result = jnp.dot(
        sigmoid_scaled.reshape(-1, expanded_dimension),
        horizontal_projector,
        preferred_element_type=jnp.float32,
    ).reshape(row_count, local_residues, channels)
    updated_rows = (homolog_tensor.astype(jnp.float32) + row_result).astype(jnp.bfloat16)
    per_device = local_residues // dap_count
    blocks = updated_rows.reshape(row_count, dap_count, per_device, channels)
    keep_blocks = keep_mask.reshape(row_count, dap_count, per_device)

    def single_column(inputs_col):
        return column_update(
            inputs_col[0],
            inputs_col[1],
            column_proj,
            vertical_projector,
            expansion_matrix,
            contraction_matrix,
        )

    column_block = lax.all_to_all(blocks, "dap", split_axis=1, concat_axis=0, tiled=True)
    column_keep = lax.all_to_all(keep_blocks, "dap", split_axis=1, concat_axis=0, tiled=True)
    inputs_col = (jnp.moveaxis(column_block[:, 0], 1, 0), jnp.moveaxis(column_keep[:, 0], 1, 0))
    output_list = lax.map(single_column, inputs_col)
    mixed = jnp.moveaxis(output_list, 0, 1)[:, None]
    returned = lax.all_to_all(mixed, "dap", split_axis=0, concat_axis=1, tiled=True)
    return returned.reshape(row_count, local_residues, channels)


def solution(mesh):
    placed = (
        P("dap", "seq", None),
        P("seq", "dap", None),
        P("dap", "seq"),
        P(),
        P(),
        P(),
        P(),
        P(),
        P(),
        P(),
        P(),
        P(),
    )
    return jax.shard_map(
        body, mesh=mesh, in_specs=placed, out_specs=P("dap", "seq", None), check_vma=False
    )
```

profile of v0, /device:TPU:0, one launch (start us, length us, event | category | flops | bytes accessed | tf_op | source)
XLA Modules:
  0.0 71.7 jit_solution(17577258312015481253)
XLA Ops:
  0.0 0.7 convert_bitcast_fusion.1
  0.7 0.7 copy.49
  1.4 5.2 %all-to-all-start.1 = ((bf16[1,8,1]{2,0,1:T(2,128)(2,1)}), bf16[1,8,1]{2,0,1:T(2,128)(2,1)S(1)}, u32[]{:S(2)}, u32[]{:S(2)}) async-start(bf16[1,8,1]{2,0,1:T(2,128)(2,1)} %copy.49), calls=%async_computation.1 | async-start | bytes 8192 | tf_op jit(solution)/shard_map/all_to_all | solution.py:151
  6.6 0.7 copy-done.12
  7.3 0.1 dynamic_slice.21
  7.3 0.1 dynamic_slice.20
  7.4 0.1 broadcast_subtract_fusion
  7.5 0.1 compare_convert_fusion
  7.6 0.5 copy-done.6
  8.0 0.1 convert_reduce_fusion.1
  8.1 0.2 fusion.38
  8.3 0.2 fusion.12
  8.6 0.6 copy-done.7
  9.2 0.7 copy-done.5
  9.9 0.1 convert_reduce_fusion
  10.0 0.2 fusion.24
  10.1 0.0 copy-start.9
  10.1 0.1 fusion.22
  10.2 0.6 copy-done.9
  10.8 0.7 copy-done.11
  11.5 0.1 fusion.13
  11.6 0.1 copy.43
  11.7 9.7 %all_gather.11 = bf16[8,8,32]{1,0,2:T(8,128)(2,1)S(1)} all-gather(bf16[8,8,4]{1,0,2:T(8,128)(2,1)S(1)} %copy.43), channel_id=1, replica_groups=mesh['dap'=8,'seq'=4] {'dap'}, dimensions={2}, use_global_device_ids=true | all-gather | bytes 4608 | tf_op jit(solution)/shard_map/all_gather | solution.py:98
  21.5 0.1 copy.44
  21.6 0.6 slice-done
  22.2 13.4 %all_gather.9 = bf16[1,32,512]{2,1,0:T(8,128)(2,1)S(1)} all-gather(bf16[1,8,512]{2,1,0:T(8,128)(2,1)S(1)} %slice-done), channel_id=1, replica_groups=mesh['dap'=8,'seq'=4] {'seq'}, dimensions={1}, use_global_device_ids=true | all-gather | bytes 40960 | tf_op jit(solution)/shard_map/all_gather | solution.py:110
  35.6 0.1 reshape.208
  35.7 0.6 slice-done.1
  36.2 0.1 reshape.207
  36.3 0.6 dynamic-slice
  37.6 0.2 dynamic-update-slice
  37.8 11.7 %all-reduce = bf16[32]{0:T(256)(128)(2,1)S(1)} all-reduce(bf16[32]{0:T(256)(128)(2,1)S(1)} %dynamic-update-slice), channel_id=1, replica_groups=mesh['dap'=8,'seq'=4] {'seq'}, use_global_device_ids=true, to_apply=%add | all-reduce | flops 32 | bytes 128
  49.5 0.1 fusion.8
  49.7 0.2 fusion.66
  49.9 0.1 reshape.206
  50.0 0.0 copy-start.3
  50.0 0.3 convolution_bitcast_fusion.1
  50.3 0.1 broadcast_in_dim.72
  50.3 0.5 copy-done.3
  50.9 0.1 copy-done.8
  51.0 0.1 fusion.19
  51.2 0.6 broadcast.220
  51.8 0.7 %reduce.5 = bf16[8,256]{1,0:T(8,128)(2,1)S(1)} reduce(bf16[8,1,1,256]{3,2,1,0:T(2,128)(2,1)S(1)} %bitcast.75, bf16[]{:T(256)} %broadcast.220), dimensions={1,2}, to_apply=%bitcast.73.reduce_sub_computation | reduce | bytes 8194
  52.5 0.6 reshape.228
  53.1 3.3 %all-to-all-start = ((bf16[8,2,128]{2,1,0:T(2,128)(2,1)}), bf16[8,2,128]{2,1,0:T(2,128)(2,1)S(1)}, u32[]{:S(2)}, u32[]{:S(2)}) async-start(bf16[8,2,128]{2,1,0:T(2,128)(2,1)} %reshape.228), calls=%async_computation | async-start | bytes 8192 | tf_op jit(solution)/shard_map/all_to_all | solution.py:150
  56.4 0.2 compare_reduce_fusion
  56.6 4.3 %all-to-all-done = bf16[8,2,128]{2,1,0:T(2,128)(2,1)S(1)} async-done(((bf16[8,2,128]{2,1,0:T(2,128)(2,1)}), bf16[8,2,128]{2,1,0:T(2,128)(2,1)S(1)}, u32[]{:S(2)}, u32[]{:S(2)}) %all-to-all-start) | async-done | bytes 4128 | tf_op jit(solution)/shard_map/all_to_all | solution.py:150
  61.0 0.1 convert_reduce_fusion.2
  61.1 0.2 fusion.40
  61.3 0.0 copy-start.4
  61.3 0.2 convolution_convert_fusion
  61.5 0.1 reshape.214
  61.6 0.1 reshape.215
  61.7 0.1 fusion.6
  61.8 0.2 fusion.67
  62.0 0.1 reshape.212
  62.1 0.2 convolution_bitcast_fusion
  62.3 0.1 reshape.216
  62.4 0.3 fusion.72
  62.7 0.2 multiply_reduce_fusion
  62.9 0.4 fusion.18
  63.3 0.7 reduce.6
  64.0 7.1 %all_to_all.12 = bf16[8,2,128]{2,1,0:T(2,128)(2,1)S(1)} all-to-all(bf16[8,2,128]{2,1,0:T(2,128)(2,1)S(1)} %reshape.230), channel_id=1, replica_groups=mesh['dap'=8,'seq'=4] {'dap'}, dimensions={0} | all-to-all | bytes 8192 | tf_op jit(solution)/shard_map/all_to_all | solution.py:155
  71.1 0.6 copy.83
  (39 shorter events, 0.2 us)
Async XLA Ops:
  0.0 8.3 %copy-start = (bf16[256,1024]{1,0:T(8,128)(2,1)S(1)}, bf16[256,1024]{1,0:T(8,128)(2,1)}, u32[]{:S(2)}) copy-start(bf16[256,1024]{1,0:T(8,128)(2,1)} %param.16) | copy-start | bytes 1572868
  1.4 51.7 %all-to-all-start.1 = ((bf16[1,8,1]{2,0,1:T(2,128)(2,1)}), bf16[1,8,1]{2,0,1:T(2,128)(2,1)S(1)}, u32[]{:S(2)}, u32[]{:S(2)}) async-start(bf16[1,8,1]{2,0,1:T(2,128)(2,1)} %copy.49), calls=%async_computation.1 | async-start | bytes 8192 | tf_op jit(solution)/shard_map/all_to_all | solution.py:151
  6.6 0.7 copy-start.12
  7.3 0.7 copy-start.6
  8.6 0.6 copy-start.7
  9.2 0.7 copy-start.5
  10.1 0.7 copy-start.9
  10.8 0.7 copy-start.11
  21.5 0.7 slice-start
  35.5 0.8 %copy-start.13 = (u32[32]{0:T(128)S(1)}, u32[32]{0:T(128)}, u32[]{:S(2)}) copy-start(u32[32]{0:T(128)} %constant.98) | copy-start | bytes 388
  35.5 0.7 slice-start.1
  35.5 25.7 %copy-start.10 = (bf16[256,1024]{1,0:T(8,128)(2,1)S(1)}, bf16[256,1024]{1,0:T(8,128)(2,1)}, u32[]{:S(2)}) copy-start(bf16[256,1024]{1,0:T(8,128)(2,1)} %param.20) | copy-start | bytes 1572868
  50.0 0.9 %copy-start.3 = (bf16[256,256]{1,0:T(8,128)(2,1)S(1)}, bf16[256,256]{1,0:T(8,128)(2,1)}, u32[]{:S(2)}) copy-start(bf16[256,256]{1,0:T(8,128)(2,1)} %param.17) | copy-start | bytes 393220
  50.3 0.7 %copy-start.8 = (bf16[1,8,1024]{2,1,0:T(8,128)(2,1)S(1)}, bf16[1,8,1024]{2,1,0:T(8,128)(2,1)}, u32[]{:S(2)}) copy-start(bf16[1,8,1024]{2,1,0:T(8,128)(2,1)} %copy-done.7) | copy-start | bytes 49156
  53.1 7.9 %all-to-all-start = ((bf16[8,2,128]{2,1,0:T(2,128)(2,1)}), bf16[8,2,128]{2,1,0:T(2,128)(2,1)S(1)}, u32[]{:S(2)}, u32[]{:S(2)}) async-start(bf16[8,2,128]{2,1,0:T(2,128)(2,1)} %reshape.228), calls=%async_computation | async-start | bytes 8192 | tf_op jit(solution)/shard_map/all_to_all | solution.py:150
  61.3 1.1 %copy-start.4 = (bf16[256,256]{1,0:T(8,128)(2,1)S(1)}, bf16[256,256]{1,0:T(8,128)(2,1)}, u32[]{:S(2)}) copy-start(bf16[256,256]{1,0:T(8,128)(2,1)} %param.21) | copy-start | bytes 393220
  61.3 1.6 %copy-start.2 = (bf16[256,1024]{1,0:T(8,128)(2,1)S(1)}, bf16[256,1024]{1,0:T(8,128)(2,1)}, u32[]{:S(2)}) copy-start(bf16[256,1024]{1,0:T(8,128)(2,1)} %param.22) | copy-start | bytes 1572868
  61.5 1.3 %copy-start.1 = (bf16[1024,256]{1,0:T(8,128)(2,1)S(1)}, bf16[1024,256]{1,0:T(8,128)(2,1)}, u32[]{:S(2)}) copy-start(bf16[1024,256]{1,0:T(8,128)(2,1)} %param.23) | copy-start | bytes 1572868
where the time goes:
time: 72.2 us; the launch traced here: 71.7 us
  blocking collectives  41.9 us (58%)
  local copies, waits for them, and re-layouts  9.98 us (14%)
  starting transfers between devices  8.51 us (12%)
  waiting for transfers between devices  4.3 us (6%)
  other arithmetic  3.88 us (5%)
  matrix products  2.23 us (3%)
  between operations  0.87 us (1%)
    all_gather x1, blocking collectives, body(): lax.all_gather(projected[..., expanded_dimension:3 * expanded_dimension],...  13.4 us
    unnamed x1, blocking collectives  11.7 us
    all_gather x1, blocking collectives, body(): pair_bias = lax.all_gather(local_bias, 'dap', axis=2, tiled=True)  9.75 us
    all_to_all x1, blocking collectives, body(): lax.all_to_all(mixed, 'dap', split_axis=0, concat_axis=1, tiled=True)  7.05 us
    unnamed x37, local copies, waits for them, and re-layouts  7.04 us
    all_to_all x1, starting transfers between devices, body(): lax.all_to_all(keep_blocks, 'dap', split_axis=1, concat_axis=0, tiled=True)  5.2 us
    all_to_all x1, waiting for transfers between devices, body(): lax.all_to_all(blocks, 'dap', split_axis=1, concat_axis=0, tiled=True)  4.3 us
    all_to_all x1, starting transfers between devices, body(): lax.all_to_all(blocks, 'dap', split_axis=1, concat_axis=0, tiled=True)  3.31 us
  transfers between devices with their start and end apart: 2, of which 1 were waited for; matrix products, arithmetic and copies ran while one was open for 8% of the time, Pallas kernels for 0%

commit v1 on v0

--- a/solution.py
+++ b/solution.py
@@ -1,6 +1,8 @@
 import jax
 import jax.numpy as jnp
 from jax import lax
+from jax.experimental import pallas as pl
+from jax.experimental.pallas import tpu as pltpu
 from jax.sharding import PartitionSpec as P
 
 HEAD_TOTAL = 8
@@ -156,6 +158,275 @@
     return returned.reshape(row_count, local_residues, channels)
 
 
+LANES = 128
+SUBLANES = 8
+WHOLE_BYTES = 1 << 20
+F32 = jnp.float32
+BF16 = jnp.bfloat16
+
+
+def mm(a, b):
+    return lax.dot_general(a, b, (((1,), (0,)), ((), ())), preferred_element_type=F32)
+
+
+def iota(shape, axis):
+    return lax.broadcasted_iota(jnp.int32, shape, axis)
+
+
+def normalize(parts, width):
+    total = parts[0]
+    for part in parts[1:]:
+        total = total + part
+    mean = jnp.sum(total, axis=-1, keepdims=True) * (1.0 / width)
+    center = [part - mean for part in parts]
+    total = center[0] * center[0]
+    for part in center[1:]:
+        total = total + part * part
+    scale = lax.rsqrt(jnp.sum(total, axis=-1, keepdims=True) * (1.0 / width) + epsilon)
+    return [part * scale for part in center]
+
+
+def halves(x):
+    return [x[:, k : k + LANES] for k in range(0, x.shape[1], LANES)]
+
+
+def normalize_rows(x):
+    return jnp.concatenate(normalize(halves(x), x.shape[1]), axis=1).astype(BF16)
+
+
+def pack_kernel(msa_ref, pair_ref, mask_ref, proj_ref, chain_ref, chain_bias_ref, out_ref):
+    queries, keys, width = pair_ref.shape
+    cells = HEAD_TOTAL * queries
+    dap, seq = lax.axis_index("dap"), lax.axis_index("seq")
+    odd = lax.rem(dap, 2)
+    spread = (iota((HEAD_TOTAL, LANES), 1) % cells // queries == iota((HEAD_TOTAL, LANES), 0)).astype(F32)
+    proj = lax.dot_general(
+        proj_ref[...], spread, (((1,), (0,)), ((), ())),
+        precision=lax.Precision.HIGHEST, preferred_element_type=F32,
+    )
+    pair = pair_ref[...].astype(F32)
+    pair = jnp.concatenate([pair, pair], axis=1).reshape(queries * 2 * keys, width)
+    normed = normalize([pair], width)[0]
+    bias = lax.dot_general(
+        normed, proj, (((1,), (0,)), ((), ())),
+        precision=lax.Precision.HIGHEST, preferred_element_type=F32,
+    ).reshape(queries, 2 * keys, LANES)
+    own = iota(bias.shape, 2) % queries == iota(bias.shape, 0)
+    bias = jnp.sum(jnp.where(own, bias, 0.0), axis=0)
+    shape = bias.shape
+    row, lane = iota(shape, 0), iota(shape, 1)
+    key_chain, query_chain = jnp.zeros(shape, jnp.int32), jnp.zeros(shape, jnp.int32)
+    for k in range(keys):
+        key_chain = jnp.where(row % keys == k, chain_ref[dap * keys + k], key_chain)
+    for k in range(queries):
+        query_chain = jnp.where(lane % queries == k, chain_ref[seq * queries + k], query_chain)
+    same, other = jnp.zeros(shape, F32), jnp.zeros(shape, F32)
+    for h in range(HEAD_TOTAL):
+        here = lane % cells // queries == h
+        same = jnp.where(here, chain_bias_ref[0, h], same)
+        other = jnp.where(here, chain_bias_ref[1, h], other)
+    bias = bias + jnp.where(key_chain == query_chain, same, other)
+    mask = jnp.zeros(shape, F32)
+    for k in range(SUBLANES):
+        mask = jnp.where(row == k, mask_ref[0, k].astype(F32), mask)
+    upper = (lane >= cells).astype(jnp.int32)
+    tail = jnp.where(upper != odd, bias, mask)
+    block = jnp.concatenate([*halves(msa_ref[0].astype(F32)), tail], axis=0).astype(BF16)
+    out_ref[...] = jnp.broadcast_to(block[None], out_ref.shape)
+
+
+def block_kernel(
+    seq_count, block_ref, row_proj_ref, row_out_ref, column_proj_ref, column_out_ref, expansion_ref,
+    contraction_ref, out_ref, normed_ref, second_ref, one_ref,
+):
+    count, rows, _ = block_ref.shape
+    own_rows = SUBLANES
+    width = rows * LANES // own_rows - LANES
+    parts = width // LANES
+    members = count // seq_count
+    residues = seq_count * own_rows
+    heads, depth = HEAD_TOTAL, HEAD_DEPTH
+    inner = heads * depth
+    cells = heads * own_rows
+    tokens = members * own_rows
+    dap, seq = lax.axis_index("dap"), lax.axis_index("seq")
+    scaling = depth**-0.5
+
+    def part(ref_index, k):
+        return block_ref[ref_index, k * own_rows : (k + 1) * own_rows, :].astype(F32)
+
+    everything = slice(None)
+    x = [part(everything, k).reshape(count * own_rows, LANES) for k in range(parts)]
+    normed = jnp.concatenate(normalize(x, width), axis=1).astype(BF16)
+    key_values = mm(normed, row_proj_ref[:, inner : 3 * inner]).astype(BF16)
+    normed_ref[...] = normed.reshape(members, seq_count, own_rows, width)
+    own = normed_ref[:, seq].reshape(tokens, width)
+    queries = mm(own, row_proj_ref[:, :inner]).astype(BF16).astype(F32)
+    gates = mm(own, row_proj_ref[:, 3 * inner :]).astype(BF16).astype(F32)
+
+    head_of = (iota((heads, 1, inner), 2) // depth == iota((heads, 1, inner), 0)).astype(F32)
+    spread = (queries.reshape(members, 1, own_rows, inner) * head_of[None]).reshape(
+        members * cells, inner
+    ).astype(BF16)
+
+    shape = (own_rows, LANES)
+    row, lane = iota(shape, 0), iota(shape, 1)
+    lower = lane < cells
+    tails = [
+        [block_ref[m * seq_count + s, parts * own_rows :, :].astype(F32) for s in range(seq_count)]
+        for m in range(members)
+    ]
+    bias = []
+    for m in range(0, members, 2):
+        even = block_ref[m * seq_count + seq, parts * own_rows :, :].astype(F32)
+        odd = block_ref[(m + 1) * seq_count + seq, parts * own_rows :, :].astype(F32)
+        first = row < own_rows // 2
+        both = jnp.where(first, even, odd)
+        bias.append(jnp.where(first != lower, both, pltpu.roll(both, cells, 1)))
+    bias = jnp.concatenate(bias, axis=0)
+    wide = iota((residues, LANES), 1) < cells
+
+    attended = []
+    for m in range(0, members, 2):
+        keys = key_values[m * residues : (m + 2) * residues, :inner]
+        values = key_values[m * residues : (m + 2) * residues, inner:]
+        scores = lax.dot_general(
+            keys, spread[m * cells : (m + 2) * cells], (((1,), (1,)), ((), ())),
+            preferred_element_type=F32,
+        )
+        scores = jnp.where(wide, scores[:residues], scores[residues:]) * scaling + bias
+        keep = jnp.concatenate(
+            [jnp.where(lower, tails[m][s], tails[m + 1][s]) for s in range(seq_count)], axis=0
+        )
+        scores = jnp.where(keep > 0, scores, -1000000000.0)
+        scores = jnp.exp(scores - jnp.max(scores, axis=0, keepdims=True))
+        weights = scores / jnp.sum(scores, axis=0, keepdims=True)
+        weights = jnp.concatenate(
+            [jnp.where(wide, weights, 0.0), jnp.where(wide, 0.0, weights)], axis=0
+        ).astype(BF16)
+        mixed = lax.dot_general(
+            weights, values, (((0,), (0,)), ((), ())), preferred_element_type=F32
+        )
+        mixed = mixed.reshape(2, heads, own_rows, inner) * head_of[None]
+        attended.append(jnp.sum(mixed, axis=1))
+    attended = jnp.concatenate(attended, axis=0).reshape(tokens, inner)
+    gated = (jax.nn.sigmoid(gates) * attended).astype(BF16)
+    residual = jnp.concatenate(
+        [
+            jnp.concatenate([part(m * seq_count + seq, k) for k in range(parts)], axis=1)
+            for m in range(members)
+        ],
+        axis=0,
+    )
+    one = (residual + mm(gated, row_out_ref[...])).astype(BF16).astype(F32)
+    one_ref[...] = one.reshape(members, own_rows, width)
+
+    second = normalize_rows(one)
+    second_ref[...] = second.reshape(members, own_rows, width)
+    key_values = mm(second, column_proj_ref[:, inner : 3 * inner]).astype(BF16).astype(F32)
+    own = second_ref[dap]
+    queries = mm(own, column_proj_ref[:, :inner]).astype(BF16).astype(F32)
+    gates = mm(own, column_proj_ref[:, 3 * inner :]).astype(BF16).astype(F32)
+    products = (
+        key_values[:, :inner].reshape(members, own_rows, inner) * queries[None]
+    ).reshape(tokens, inner)
+    high = products.astype(BF16)
+    low = (products - high.astype(F32)).astype(BF16)
+    same_head = (iota((inner, inner), 0) // depth == iota((inner, inner), 1) // depth).astype(
+        F32
+    ).astype(BF16)
+    scores = (mm(high, same_head) + mm(low, same_head)) * scaling
+    scores = scores.reshape(members, own_rows, inner)
+    keep = []
+    for m in range(members):
+        tail = block_ref[m * seq_count + seq, parts * own_rows :, :].astype(F32)
+        mine = lower if m % 2 == 0 else jnp.logical_not(lower)
+        tail = jnp.where(mine, tail, pltpu.roll(tail, cells, 1))
+        keep.append(jnp.concatenate([tail] * (inner // LANES), axis=1)[None])
+    keep = jnp.concatenate(keep, axis=0)
+    scores = jnp.where(keep > 0, scores, -1000000000.0)
+    scores = jnp.exp(scores - jnp.max(scores, axis=0, keepdims=True))
+    weights = (scores / jnp.sum(scores, axis=0, keepdims=True)).astype(BF16).astype(F32)
+    attended = jnp.sum(
+        weights * key_values[:, inner:].reshape(members, own_rows, inner), axis=0
+    )
+    gated = (jax.nn.sigmoid(gates) * attended).astype(BF16)
+    two = one_ref[dap] + mm(gated, column_out_ref[...])
+    hidden = jnp.maximum(mm(normalize_rows(two), expansion_ref[...]), 0.0).astype(BF16)
+    out_ref[0] = (two + mm(hidden, contraction_ref[...])).astype(BF16)
+
+
+def whole_body(
+    homolog_tensor,
+    pair_features,
+    entry_real_mask,
+    chain_ids,
+    horizontal_matrices,
+    horizontal_projector,
+    bias_proj,
+    chain_bias,
+    column_proj,
+    vertical_projector,
+    expansion_matrix,
+    contraction_matrix,
+):
+    _, own_rows, width = homolog_tensor.shape
+    dap_count, seq_count = lax.axis_size("dap"), lax.axis_size("seq")
+    count = dap_count * seq_count
+    rows = own_rows * (width // LANES + 1)
+    vmem, smem = (pl.BlockSpec(memory_space=space) for space in (pltpu.VMEM, pltpu.SMEM))
+    packed = pl.pallas_call(
+        pack_kernel,
+        out_shape=jax.ShapeDtypeStruct((count, rows, LANES), BF16),
+        in_specs=[vmem, vmem, smem, vmem, smem, smem],
+        out_specs=vmem,
+        compiler_params=pltpu.CompilerParams(vmem_limit_bytes=8 << 20),
+    )(homolog_tensor, pair_features, entry_real_mask, bias_proj, chain_ids, chain_bias)
+    blocks = lax.all_to_all(packed, ("dap", "seq"), split_axis=0, concat_axis=0, tiled=True)
+    return pl.pallas_call(
+        lambda *refs: block_kernel(seq_count, *refs),
+        out_shape=jax.ShapeDtypeStruct(homolog_tensor.shape, BF16),
+        in_specs=[vmem] * 7,
+        out_specs=vmem,
+        scratch_shapes=[
+            pltpu.VMEM((dap_count, seq_count, own_rows, width), BF16),
+            pltpu.VMEM((dap_count, own_rows, width), BF16),
+            pltpu.VMEM((dap_count, own_rows, width), F32),
+        ],
+        compiler_params=pltpu.CompilerParams(vmem_limit_bytes=16 << 20),
+    )(
+        blocks,
+        horizontal_matrices,
+        horizontal_projector,
+        column_proj,
+        vertical_projector,
+        expansion_matrix,
+        contraction_matrix,
+    )
+
+
+def fits_whole(homolog_tensor, pair_features, dap_count):
+    row_count, local_residues, width = homolog_tensor.shape
+    queries, keys, pair_width = pair_features.shape
+    return (
+        row_count == 1
+        and local_residues == SUBLANES
+        and queries == local_residues
+        and 2 * keys == SUBLANES
+        and dap_count % 2 == 0
+        and 2 * HEAD_TOTAL * queries == LANES
+        and width % LANES == 0
+        and pair_width == LANES
+        and HEAD_TOTAL * HEAD_DEPTH % LANES == 0
+        and lax.axis_size("seq") * dap_count * homolog_tensor.size * 2 <= WHOLE_BYTES
+    )
+
+
+def choose(*operands):
+    whole = fits_whole(operands[0], operands[1], lax.axis_size("dap"))
+    return whole_body(*operands) if whole else body(*operands)
+
+
 def solution(mesh):
     placed = (
         P("dap", "seq", None),
@@ -172,5 +443,5 @@
         P(),
     )
     return jax.shard_map(
-        body, mesh=mesh, in_specs=placed, out_specs=P("dap", "seq", None), check_vma=False
-    )
+        choose, mesh=mesh, in_specs=placed, out_specs=P("dap", "seq", None), check_vma=False
+    )

time: 72.2 us -> 26.1 us (0.36)
  blocking collectives: 41.9 us -> 16.4 us
  starting transfers between devices: 8.51 us -> 0 us
  local copies, waits for them, and re-layouts: 9.98 us -> 4.91 us
  Pallas kernels: 0 us -> 4.34 us
  waiting for transfers between devices: 4.3 us -> 0 us
  other arithmetic: 3.88 us -> 0 us
  matrix products: 2.23 us -> 0 us
  between operations: 0.87 us -> 0.07 us
    all_gather x2 -> x0, blocking collectives: 23.1 us -> none  [the longest x1 13.4 us: body(): lax.all_gather(projected[..., expanded_dimension:3 * expanded_dimension],...]
    unnamed x1 -> x0, blocking collectives: 11.7 us -> none
    all_to_all x1, blocking collectives: 7.05 us -> 16.4 us  [whole_body(): lax.all_to_all(packed, ('dap', 'seq'), split_axis=0, concat_axis=0, tiled...]
    all_to_all x2 -> x0, starting transfers between devices: 8.51 us -> none  [the longest x1 5.2 us: body(): lax.all_to_all(keep_blocks, 'dap', split_axis=1, concat_axis=0, tiled=True)]
    pallas_call x0 -> x2, Pallas kernels: none -> 4.34 us  [the longest x1 3.34 us: whole_body(): pl.pallas_call(lambda *refs: block_kernel(seq_count, *refs), out_shape=ja...]
    all_to_all x2 -> x0, waiting for transfers between devices: 4.3 us -> none  [the longest x1 4.3 us: body(): lax.all_to_all(blocks, 'dap', split_axis=1, concat_axis=0, tiled=True)]
    unnamed x37 -> x23, local copies, waits for them, and re-layouts: 7.04 us -> 4.91 us
    dot_general x10 -> x0, matrix products: 2.07 us -> none  [the longest x2 0.46 us: attend(): jnp.einsum('hij,jhd->ihd', weights, value_part, preferred_element_type=jn...]
  transfers between devices with their start and end apart: 2 -> 0, of which waited for: 1 -> 0; matrix products, arithmetic and copies ran while one was open for 8% -> 0% of each run, Pallas kernels for 0% -> 0%
where the time goes in v1:
time: 26.1 us; the launch traced here: 25.8 us
  blocking collectives  16.4 us (63%)
  local copies, waits for them, and re-layouts  4.91 us (19%)
  Pallas kernels  4.34 us (17%)
    all_to_all x1, blocking collectives, whole_body(): lax.all_to_all(packed, ('dap', 'seq'), split_axis=0, concat_axis=0, tiled...  16.4 us
    unnamed x23, local copies, waits for them, and re-layouts  4.91 us
    pallas_call x1, Pallas kernels, whole_body(): pl.pallas_call(lambda *refs: block_kernel(seq_count, *refs), out_shape=ja...  3.34 us
    pallas_call x1, Pallas kernels, whole_body(): pl.pallas_call(pack_kernel, out_shape=jax.ShapeDtypeStruct((count, rows,...  1 us

profile of v1, /device:TPU:0, one launch (start us, length us, event | category | flops | bytes accessed | tf_op | source)
XLA Modules:
  0.0 25.8 jit_solution(9725466021550544281)
XLA Ops:
  0.0 0.0 copy-start.8
  0.0 0.0 copy-start.10
  0.0 0.0 copy-start.9
  0.0 0.0 copy-start.6
  0.0 0.0 copy-start.7
  0.0 0.0 copy-start
  0.0 0.9 %copy.13.proj_ref = f32[128,8]{1,0:T(8,128)S(1)} copy(f32[128,8]{0,1:T(8,128)} %param.18) | data formatting | bytes 8192 | tf_op args[6]
  0.9 0.0 copy-done.8
  0.9 0.0 copy-done.10
  0.9 0.0 copy-done.9
  0.9 0.0 copy-done.6
  0.9 0.0 copy-done.7
  0.9 1.0 %shard_map.118 = bf16[32,24,128]{2,1,0:T(8,128)(2,1)S(1)} custom-call(bf16[1,8,256]{2,1,0:T(8,128)(2,1)S(1)} %copy-done.7, bf16[8,4,128]{2,1,0:T(4,128)(2,1)S(1)} %copy-done.6, s32[1,8]{1,0:T(1,128)S(1)} %copy-done.9, f32[128,8]{1,0:T(8,128)S(1)} %copy.13.proj_ref, s32[32]{0:T(128)S(1)} %copy-done.10, f32[2,8]{1,0:T(2,128)S(1)} %copy-done.8), custom_call_target="tpu_custom_call" | custom-call | tf_op jit(solution)/shard_map/pallas_call | solution.py:378
  1.9 0.0 copy-start.4
  1.9 16.4 %all_to_all.5.refs_0_ = bf16[32,24,128]{2,1,0:T(8,128)(2,1)S(1)} all-to-all(bf16[32,24,128]{2,1,0:T(8,128)(2,1)S(1)} %shard_map.118), channel_id=1, replica_groups=mesh['dap'=8,'seq'=4] {'dap','seq'}, dimensions={0} | all-to-all | bytes 393216 | tf_op jit(solution)/shard_map/all_to_all | solution.py:385
  18.4 0.0 copy-done
  18.4 0.0 copy-done.4
  18.4 0.0 copy-start.1
  18.4 1.0 %copy-done.1 = bf16[256,1024]{1,0:T(8,128)(2,1)S(1)} copy-done((bf16[256,1024]{1,0:T(8,128)(2,1)S(1)}, bf16[256,1024]{1,0:T(8,128)(2,1)}, u32[]{:S(2)}) %copy-start.1) | copy-done | bytes 524312
  19.4 0.0 copy-start.2
  19.4 1.0 %copy-done.2 = bf16[256,1024]{1,0:T(8,128)(2,1)S(1)} copy-done((bf16[256,1024]{1,0:T(8,128)(2,1)S(1)}, bf16[256,1024]{1,0:T(8,128)(2,1)}, u32[]{:S(2)}) %copy-start.2) | copy-done | bytes 524312
  20.5 0.0 copy-start.3
  20.5 1.0 %copy-done.3 = bf16[1024,256]{1,0:T(8,128)(2,1)S(1)} copy-done((bf16[1024,256]{1,0:T(8,128)(2,1)S(1)}, bf16[1024,256]{1,0:T(8,128)(2,1)}, u32[]{:S(2)}) %copy-start.3) | copy-done | bytes 524312
  21.5 0.0 copy-start.5
  21.5 0.9 %copy-done.5 = bf16[256,256]{1,0:T(8,128)(2,1)S(1)} copy-done((bf16[256,256]{1,0:T(8,128)(2,1)S(1)}, bf16[256,256]{1,0:T(8,128)(2,1)}, u32[]{:S(2)}) %copy-start.5) | copy-done | bytes 131096
  22.4 3.3 %shard_map.119 = bf16[1,8,256]{2,1,0:T(8,128)(2,1)} custom-call(bf16[32,24,128]{2,1,0:T(8,128)(2,1)S(1)} %all_to_all.5.refs_0_, bf16[256,1024]{1,0:T(8,128)(2,1)S(1)} %copy-done, bf16[256,256]{1,0:T(8,128)(2,1)S(1)} %copy-done.4, bf16[256,1024]{1,0:T(8,128)(2,1)S(1)} %copy-done.1, bf16[256,256]{1,0:T(8,128)(2,1)S(1)} %copy-done.5, ...), custom_call_target="tpu_custom_call" | custom-call | tf_op jit(solution)/shard_map/pallas_call | solution.py:386
Async XLA Ops:
  0.0 0.9 %copy-start.8 = (f32[2,8]{1,0:T(2,128)S(1)}, f32[2,8]{1,0:T(2,128)}, u32[]{:S(2)}) copy-start(f32[2,8]{1,0:T(2,128)} %chain_bias_ref.1) | copy-start | bytes 196
  0.0 0.9 %copy-start.10 = (s32[32]{0:T(128)S(1)}, s32[32]{0:T(128)}, u32[]{:S(2)}) copy-start(s32[32]{0:T(128)} %chain_ref.1) | copy-start | bytes 388
  0.0 0.9 %copy-start.9 = (s32[1,8]{1,0:T(1,128)S(1)}, s32[1,8]{1,0:T(1,128)}, u32[]{:S(2)}) copy-start(s32[1,8]{1,0:T(1,128)} %mask_ref.1) | copy-start | bytes 100
  0.0 0.9 %copy-start.6 = (bf16[8,4,128]{2,1,0:T(4,128)(2,1)S(1)}, bf16[8,4,128]{2,1,0:T(4,128)(2,1)}, u32[]{:S(2)}) copy-start(bf16[8,4,128]{2,1,0:T(4,128)(2,1)} %pair_ref.1) | copy-start | bytes 24580
  0.0 0.9 %copy-start.7 = (bf16[1,8,256]{2,1,0:T(8,128)(2,1)S(1)}, bf16[1,8,256]{2,1,0:T(8,128)(2,1)}, u32[]{:S(2)}) copy-start(bf16[1,8,256]{2,1,0:T(8,128)(2,1)} %msa_ref.1) | copy-start | bytes 12292
  0.0 18.4 %copy-start = (bf16[256,1024]{1,0:T(8,128)(2,1)S(1)}, bf16[256,1024]{1,0:T(8,128)(2,1)}, u32[]{:S(2)}) copy-start(bf16[256,1024]{1,0:T(8,128)(2,1)} %refs_1_.1) | copy-start | bytes 1572868
  1.9 16.5 %copy-start.4 = (bf16[256,256]{1,0:T(8,128)(2,1)S(1)}, bf16[256,256]{1,0:T(8,128)(2,1)}, u32[]{:S(2)}) copy-start(bf16[256,256]{1,0:T(8,128)(2,1)} %refs_2_.1) | copy-start | bytes 393220
  18.4 1.0 %copy-start.1 = (bf16[256,1024]{1,0:T(8,128)(2,1)S(1)}, bf16[256,1024]{1,0:T(8,128)(2,1)}, u32[]{:S(2)}) copy-start(bf16[256,1024]{1,0:T(8,128)(2,1)} %refs_3_.1) | copy-start | bytes 1572868
  19.4 1.0 %copy-start.2 = (bf16[256,1024]{1,0:T(8,128)(2,1)S(1)}, bf16[256,1024]{1,0:T(8,128)(2,1)}, u32[]{:S(2)}) copy-start(bf16[256,1024]{1,0:T(8,128)(2,1)} %refs_5_.1) | copy-start | bytes 1572868
  20.5 1.0 %copy-start.3 = (bf16[1024,256]{1,0:T(8,128)(2,1)S(1)}, bf16[1024,256]{1,0:T(8,128)(2,1)}, u32[]{:S(2)}) copy-start(bf16[1024,256]{1,0:T(8,128)(2,1)} %refs_6_.1) | copy-start | bytes 1572868
  21.5 0.9 %copy-start.5 = (bf16[256,256]{1,0:T(8,128)(2,1)S(1)}, bf16[256,256]{1,0:T(8,128)(2,1)}, u32[]{:S(2)}) copy-start(bf16[256,256]{1,0:T(8,128)(2,1)} %refs_4_.1) | copy-start | bytes 393220

commit v2 on v1

--- a/solution.py
+++ b/solution.py
@@ -194,38 +194,51 @@
     return jnp.concatenate(normalize(halves(x), x.shape[1]), axis=1).astype(BF16)
 
 
-def pack_kernel(msa_ref, pair_ref, mask_ref, proj_ref, chain_ref, chain_bias_ref, out_ref):
+def pack_kernel(*refs):
+    count = (len(refs) - 2) // 2
+    out_ref, arrived = refs[count], refs[-1]
+    near = refs[count + 1 : -1]
+    copies = [
+        pltpu.make_async_copy(source, target, arrived.at[k])
+        for k, (source, target) in enumerate(zip(refs[:count], near))
+    ]
+    for copy in copies:
+        copy.start()
+    for copy in copies:
+        copy.wait()
+    pair_ref, proj_ref, msa_ref, chain_ref, chain_bias_ref, mask_ref = near
     queries, keys, width = pair_ref.shape
     cells = HEAD_TOTAL * queries
     dap, seq = lax.axis_index("dap"), lax.axis_index("seq")
     odd = lax.rem(dap, 2)
-    spread = (iota((HEAD_TOTAL, LANES), 1) % cells // queries == iota((HEAD_TOTAL, LANES), 0)).astype(F32)
-    proj = lax.dot_general(
-        proj_ref[...], spread, (((1,), (0,)), ((), ())),
+    pairs = queries * keys
+    normed = normalize([pair_ref[...].astype(F32).reshape(pairs, width)], width)[0]
+    bias = lax.dot_general(
+        proj_ref[...], normed, (((1,), (1,)), ((), ())),
         precision=lax.Precision.HIGHEST, preferred_element_type=F32,
     )
-    pair = pair_ref[...].astype(F32)
-    pair = jnp.concatenate([pair, pair], axis=1).reshape(queries * 2 * keys, width)
-    normed = normalize([pair], width)[0]
+    shape = bias.shape
+    head, pair = iota(shape, 0), iota(shape, 1)
+    key_chain, query_chain = jnp.zeros(shape, jnp.int32), jnp.zeros(shape, jnp.int32)
+    for k in range(keys):
+        key_chain = jnp.where(pair % keys == k, chain_ref[dap * keys + k], key_chain)
+    for k in range(queries):
+        query_chain = jnp.where(pair // keys == k, chain_ref[seq * queries + k], query_chain)
+    same, other = jnp.zeros(shape, F32), jnp.zeros(shape, F32)
+    for h in range(HEAD_TOTAL):
+        same = jnp.where(head == h, chain_bias_ref[0, h], same)
+        other = jnp.where(head == h, chain_bias_ref[1, h], other)
+    bias = (bias + jnp.where(key_chain == query_chain, same, other)).astype(BF16)
+    heads = (iota((HEAD_TOTAL, LANES), 1) % cells // queries == iota((HEAD_TOTAL, LANES), 0)).astype(F32)
     bias = lax.dot_general(
-        normed, proj, (((1,), (0,)), ((), ())),
-        precision=lax.Precision.HIGHEST, preferred_element_type=F32,
-    ).reshape(queries, 2 * keys, LANES)
-    own = iota(bias.shape, 2) % queries == iota(bias.shape, 0)
-    bias = jnp.sum(jnp.where(own, bias, 0.0), axis=0)
+        bias, heads.astype(BF16), (((0,), (0,)), ((), ())), preferred_element_type=F32
+    )
+    own = iota(bias.shape, 1) % queries == iota(bias.shape, 0) // keys
+    bias = jnp.where(own, bias, 0.0).reshape(pairs // SUBLANES, SUBLANES, LANES)
+    bias = jnp.sum(bias, axis=0)
+    bias = bias + pltpu.roll(bias, keys, 0)
     shape = bias.shape
     row, lane = iota(shape, 0), iota(shape, 1)
-    key_chain, query_chain = jnp.zeros(shape, jnp.int32), jnp.zeros(shape, jnp.int32)
-    for k in range(keys):
-        key_chain = jnp.where(row % keys == k, chain_ref[dap * keys + k], key_chain)
-    for k in range(queries):
-        query_chain = jnp.where(lane % queries == k, chain_ref[seq * queries + k], query_chain)
-    same, other = jnp.zeros(shape, F32), jnp.zeros(shape, F32)
-    for h in range(HEAD_TOTAL):
-        here = lane % cells // queries == h
-        same = jnp.where(here, chain_bias_ref[0, h], same)
-        other = jnp.where(here, chain_bias_ref[1, h], other)
-    bias = bias + jnp.where(key_chain == query_chain, same, other)
     mask = jnp.zeros(shape, F32)
     for k in range(SUBLANES):
         mask = jnp.where(row == k, mask_ref[0, k].astype(F32), mask)
@@ -236,9 +249,20 @@
 
 
 def block_kernel(
-    seq_count, block_ref, row_proj_ref, row_out_ref, column_proj_ref, column_out_ref, expansion_ref,
-    contraction_ref, out_ref, normed_ref, second_ref, one_ref,
+    seq_count, block_ref, row_proj_ref, row_out_far, column_proj_far, column_out_far, expansion_far,
+    contraction_far, out_ref, second_ref, one_ref, row_out_ref, column_proj_ref,
+    column_out_ref, expansion_ref, contraction_ref, arrived, fence,
 ):
+    far = (row_out_far, column_proj_far, column_out_far, expansion_far, contraction_far)
+    near = (row_out_ref, column_proj_ref, column_out_ref, expansion_ref, contraction_ref)
+    copies = [
+        pltpu.make_async_copy(source, target, arrived.at[k])
+        for k, (source, target) in enumerate(zip(far, near))
+    ]
+    for copy in copies:
+        copy.start()
+    pl.semaphore_signal(fence, 1)
+    pl.semaphore_wait(fence, 1)
     count, rows, _ = block_ref.shape
     own_rows = SUBLANES
     width = rows * LANES // own_rows - LANES
@@ -255,74 +279,81 @@
     def part(ref_index, k):
         return block_ref[ref_index, k * own_rows : (k + 1) * own_rows, :].astype(F32)
 
+    def tail(m, s):
+        return block_ref[m * seq_count + s, parts * own_rows :, :].astype(F32)
+
+    def mine(k):
+        return jnp.concatenate([part(m * seq_count + seq, k) for m in range(members)], axis=0)
+
+    residual = [mine(k) for k in range(parts)]
+    own = jnp.concatenate(normalize(residual, width), axis=1).astype(BF16)
+    queries = mm(own, row_proj_ref[:, :inner]).astype(BF16).astype(F32)
+    gates = mm(own, row_proj_ref[:, 3 * inner :]).astype(BF16).astype(F32)
     everything = slice(None)
     x = [part(everything, k).reshape(count * own_rows, LANES) for k in range(parts)]
     normed = jnp.concatenate(normalize(x, width), axis=1).astype(BF16)
-    key_values = mm(normed, row_proj_ref[:, inner : 3 * inner]).astype(BF16)
-    normed_ref[...] = normed.reshape(members, seq_count, own_rows, width)
-    own = normed_ref[:, seq].reshape(tokens, width)
-    queries = mm(own, row_proj_ref[:, :inner]).astype(BF16).astype(F32)
-    gates = mm(own, row_proj_ref[:, 3 * inner :]).astype(BF16).astype(F32)
-
-    head_of = (iota((heads, 1, inner), 2) // depth == iota((heads, 1, inner), 0)).astype(F32)
-    spread = (queries.reshape(members, 1, own_rows, inner) * head_of[None]).reshape(
-        members * cells, inner
-    ).astype(BF16)
+    all_keys = mm(normed, row_proj_ref[:, inner : 2 * inner]).astype(BF16)
+    all_values = mm(normed, row_proj_ref[:, 2 * inner : 3 * inner]).astype(BF16)
+
+    head_of = iota((heads, 1, inner), 2) // depth == iota((heads, 1, inner), 0)
+    spread = jnp.where(
+        head_of[None], queries.reshape(members, 1, own_rows, inner), 0.0
+    ).reshape(members * cells, inner).astype(BF16)
 
     shape = (own_rows, LANES)
     row, lane = iota(shape, 0), iota(shape, 1)
     lower = lane < cells
-    tails = [
-        [block_ref[m * seq_count + s, parts * own_rows :, :].astype(F32) for s in range(seq_count)]
-        for m in range(members)
-    ]
     bias = []
     for m in range(0, members, 2):
-        even = block_ref[m * seq_count + seq, parts * own_rows :, :].astype(F32)
-        odd = block_ref[(m + 1) * seq_count + seq, parts * own_rows :, :].astype(F32)
         first = row < own_rows // 2
-        both = jnp.where(first, even, odd)
+        both = jnp.where(first, tail(m, seq), tail(m + 1, seq))
         bias.append(jnp.where(first != lower, both, pltpu.roll(both, cells, 1)))
     bias = jnp.concatenate(bias, axis=0)
     wide = iota((residues, LANES), 1) < cells
-
-    attended = []
-    for m in range(0, members, 2):
-        keys = key_values[m * residues : (m + 2) * residues, :inner]
-        values = key_values[m * residues : (m + 2) * residues, inner:]
-        scores = lax.dot_general(
-            keys, spread[m * cells : (m + 2) * cells], (((1,), (1,)), ((), ())),
+    keeps = [
+        jnp.concatenate(
+            [jnp.where(lower, tail(m, s), tail(m + 1, s)) for s in range(seq_count)], axis=0
+        ) > 0
+        for m in range(0, members, 2)
+    ]
+
+    scores = [
+        lax.dot_general(
+            all_keys[m * residues : (m + 2) * residues],
+            spread[m * cells : (m + 2) * cells],
+            (((1,), (1,)), ((), ())),
             preferred_element_type=F32,
         )
-        scores = jnp.where(wide, scores[:residues], scores[residues:]) * scaling + bias
-        keep = jnp.concatenate(
-            [jnp.where(lower, tails[m][s], tails[m + 1][s]) for s in range(seq_count)], axis=0
+        for m in range(0, members, 2)
+    ]
+    scores = [jnp.where(wide, two[:residues], two[residues:]) * scaling + bias for two in scores]
+    scores = [jnp.where(keep, two, -1000000000.0) for two, keep in zip(scores, keeps)]
+    scores = [jnp.exp(two - jnp.max(two, axis=0, keepdims=True)) for two in scores]
+    weights = [two / jnp.sum(two, axis=0, keepdims=True) for two in scores]
+    weights = [
+        jnp.concatenate([jnp.where(wide, two, 0.0), jnp.where(wide, 0.0, two)], axis=0).astype(BF16)
+        for two in weights
+    ]
+    mixed = [
+        lax.dot_general(
+            two, all_values[2 * k * residues : 2 * (k + 1) * residues],
+            (((0,), (0,)), ((), ())), preferred_element_type=F32,
         )
-        scores = jnp.where(keep > 0, scores, -1000000000.0)
-        scores = jnp.exp(scores - jnp.max(scores, axis=0, keepdims=True))
-        weights = scores / jnp.sum(scores, axis=0, keepdims=True)
-        weights = jnp.concatenate(
-            [jnp.where(wide, weights, 0.0), jnp.where(wide, 0.0, weights)], axis=0
-        ).astype(BF16)
-        mixed = lax.dot_general(
-            weights, values, (((0,), (0,)), ((), ())), preferred_element_type=F32
-        )
-        mixed = mixed.reshape(2, heads, own_rows, inner) * head_of[None]
-        attended.append(jnp.sum(mixed, axis=1))
-    attended = jnp.concatenate(attended, axis=0).reshape(tokens, inner)
+        for k, two in enumerate(weights)
+    ]
+    mixed = [
+        jnp.sum(jnp.where(head_of[None], two.reshape(2, heads, own_rows, inner), 0.0), axis=1)
+        for two in mixed
+    ]
+    attended = jnp.concatenate(mixed, axis=0).reshape(tokens, inner)
     gated = (jax.nn.sigmoid(gates) * attended).astype(BF16)
-    residual = jnp.concatenate(
-        [
-            jnp.concatenate([part(m * seq_count + seq, k) for k in range(parts)], axis=1)
-            for m in range(members)
-        ],
-        axis=0,
-    )
-    one = (residual + mm(gated, row_out_ref[...])).astype(BF16).astype(F32)
+    copies[0].wait()
+    one = (jnp.concatenate(residual, axis=1) + mm(gated, row_out_ref[...])).astype(BF16).astype(F32)
     one_ref[...] = one.reshape(members, own_rows, width)
 
     second = normalize_rows(one)
     second_ref[...] = second.reshape(members, own_rows, width)
+    copies[1].wait()
     key_values = mm(second, column_proj_ref[:, inner : 3 * inner]).astype(BF16).astype(F32)
     own = second_ref[dap]
     queries = mm(own, column_proj_ref[:, :inner]).astype(BF16).astype(F32)
@@ -339,10 +370,10 @@
     scores = scores.reshape(members, own_rows, inner)
     keep = []
     for m in range(members):
-        tail = block_ref[m * seq_count + seq, parts * own_rows :, :].astype(F32)
-        mine = lower if m % 2 == 0 else jnp.logical_not(lower)
-        tail = jnp.where(mine, tail, pltpu.roll(tail, cells, 1))
-        keep.append(jnp.concatenate([tail] * (inner // LANES), axis=1)[None])
+        mask = tail(m, seq)
+        valid = lower if m % 2 == 0 else jnp.logical_not(lower)
+        mask = jnp.where(valid, mask, pltpu.roll(mask, cells, 1))
+        keep.append(jnp.concatenate([mask] * (inner // LANES), axis=1)[None])
     keep = jnp.concatenate(keep, axis=0)
     scores = jnp.where(keep > 0, scores, -1000000000.0)
     scores = jnp.exp(scores - jnp.max(scores, axis=0, keepdims=True))
@@ -351,8 +382,11 @@
         weights * key_values[:, inner:].reshape(members, own_rows, inner), axis=0
     )
     gated = (jax.nn.sigmoid(gates) * attended).astype(BF16)
+    copies[2].wait()
     two = one_ref[dap] + mm(gated, column_out_ref[...])
+    copies[3].wait()
     hidden = jnp.maximum(mm(normalize_rows(two), expansion_ref[...]), 0.0).astype(BF16)
+    copies[4].wait()
     out_ref[0] = (two + mm(hidden, contraction_ref[...])).astype(BF16)
 
 
@@ -374,35 +408,43 @@
     dap_count, seq_count = lax.axis_size("dap"), lax.axis_size("seq")
     count = dap_count * seq_count
     rows = own_rows * (width // LANES + 1)
-    vmem, smem = (pl.BlockSpec(memory_space=space) for space in (pltpu.VMEM, pltpu.SMEM))
+    vmem, hbm = (pl.BlockSpec(memory_space=space) for space in (pltpu.VMEM, pltpu.HBM))
+    vectors = [pair_features, bias_proj.T, homolog_tensor]
+    scalars = [chain_ids, chain_bias, entry_real_mask]
     packed = pl.pallas_call(
         pack_kernel,
         out_shape=jax.ShapeDtypeStruct((count, rows, LANES), BF16),
-        in_specs=[vmem, vmem, smem, vmem, smem, smem],
+        in_specs=[hbm] * len(vectors + scalars),
         out_specs=vmem,
+        scratch_shapes=[
+            *(pltpu.VMEM(operand.shape, operand.dtype) for operand in vectors),
+            *(pltpu.SMEM(operand.shape, operand.dtype) for operand in scalars),
+            pltpu.SemaphoreType.DMA((len(vectors + scalars),)),
+        ],
         compiler_params=pltpu.CompilerParams(vmem_limit_bytes=8 << 20),
-    )(homolog_tensor, pair_features, entry_real_mask, bias_proj, chain_ids, chain_bias)
+    )(*map(in_hbm, vectors + scalars))
     blocks = lax.all_to_all(packed, ("dap", "seq"), split_axis=0, concat_axis=0, tiled=True)
+    later = [
+        horizontal_projector, column_proj, vertical_projector, expansion_matrix, contraction_matrix
+    ]
     return pl.pallas_call(
         lambda *refs: block_kernel(seq_count, *refs),
         out_shape=jax.ShapeDtypeStruct(homolog_tensor.shape, BF16),
-        in_specs=[vmem] * 7,
+        in_specs=[vmem] * 2 + [hbm] * len(later),
         out_specs=vmem,
         scratch_shapes=[
-            pltpu.VMEM((dap_count, seq_count, own_rows, width), BF16),
             pltpu.VMEM((dap_count, own_rows, width), BF16),
             pltpu.VMEM((dap_count, own_rows, width), F32),
+            *(pltpu.VMEM(weight.shape, weight.dtype) for weight in later),
+            pltpu.SemaphoreType.DMA((len(later),)),
+            pltpu.SemaphoreType.REGULAR,
         ],
         compiler_params=pltpu.CompilerParams(vmem_limit_bytes=16 << 20),
-    )(
-        blocks,
-        horizontal_matrices,
-        horizontal_projector,
-        column_proj,
-        vertical_projector,
-        expansion_matrix,
-        contraction_matrix,
-    )
+    )(blocks, horizontal_matrices, *map(in_hbm, later))
+
+
+def in_hbm(operand):
+    return pltpu.with_memory_space_constraint(operand, pltpu.HBM)
 
 
 def fits_whole(homolog_tensor, pair_features, dap_count):

time: 26.1 us -> 20.9 us (0.80)
  local copies, waits for them, and re-layouts: 4.91 us -> 0.01 us
    unnamed x23 -> x2, local copies, waits for them, and re-layouts: 4.91 us -> 0.01 us
    pallas_call x1, Pallas kernels: 3.34 us -> 2.94 us  [whole_body(): pl.pallas_call(lambda *refs: block_kernel(seq_count, *refs), out_shape=ja...]
    pallas_call x1, Pallas kernels: 1 us -> 1.39 us  [whole_body(): pl.pallas_call(pack_kernel, out_shape=jax.ShapeDtypeStruct((count, rows,...]
where the time goes in v2:
time: 20.9 us; the launch traced here: 20.8 us
  blocking collectives  16.4 us (78%)
  Pallas kernels  4.33 us (21%)
    all_to_all x1, blocking collectives, whole_body(): lax.all_to_all(packed, ('dap', 'seq'), split_axis=0, concat_axis=0, tiled...  16.4 us
    pallas_call x1, Pallas kernels, whole_body(): pl.pallas_call(lambda *refs: block_kernel(seq_count, *refs), out_shape=ja...  2.94 us
    pallas_call x1, Pallas kernels, whole_body(): pl.pallas_call(pack_kernel, out_shape=jax.ShapeDtypeStruct((count, rows,...  1.39 us

profile of v2, /device:TPU:0, one launch (start us, length us, event | category | flops | bytes accessed | tf_op | source)
XLA Modules:
  0.0 20.8 jit_solution(6058128349437958157)
XLA Ops:
  0.0 0.0 copy-start
  0.0 1.4 %shard_map.118 = bf16[32,24,128]{2,1,0:T(8,128)(2,1)S(1)} custom-call(bf16[8,4,128]{2,1,0:T(4,128)(2,1)} %refs_0_.1, f32[8,128]{1,0:T(8,128)} %bitcast.1, bf16[1,8,256]{2,1,0:T(8,128)(2,1)} %refs_2_.2, s32[32]{0:T(128)} %refs_3_.2, f32[2,8]{1,0:T(2,128)} %refs_4_.2, s32[1,8]{1,0:T(1,128)} %refs_5_.2), custom_call_target="tpu_custom_call" | custom-call | tf_op jit(solution)/shard_map/pallas_call | solution.py:414
  1.4 16.4 %all_to_all.5.refs_0_ = bf16[32,24,128]{2,1,0:T(8,128)(2,1)S(1)} all-to-all(bf16[32,24,128]{2,1,0:T(8,128)(2,1)S(1)} %shard_map.118), channel_id=1, replica_groups=mesh['dap'=8,'seq'=4] {'dap','seq'}, dimensions={0} | all-to-all | bytes 393216 | tf_op jit(solution)/shard_map/all_to_all | solution.py:426
  17.8 0.0 copy-done
  17.8 2.9 %shard_map.119 = bf16[1,8,256]{2,1,0:T(8,128)(2,1)} custom-call(bf16[32,24,128]{2,1,0:T(8,128)(2,1)S(1)} %all_to_all.5.refs_0_, bf16[256,1024]{1,0:T(8,128)(2,1)S(1)} %copy-done, bf16[256,256]{1,0:T(8,128)(2,1)} %refs_2_.3, bf16[256,1024]{1,0:T(8,128)(2,1)} %refs_3_.3, bf16[256,256]{1,0:T(8,128)(2,1)} %refs_4_.3, bf16[256,1024]{1,0:T(8,128)(2,1)} %refs_5_.3, ...), custom_call_target="tpu_custom_call" | custom-call | tf_op jit(solution)/shard_map/pallas_call | solution.py:430
Async XLA Ops:
  0.0 17.8 %copy-start = (bf16[256,1024]{1,0:T(8,128)(2,1)S(1)}, bf16[256,1024]{1,0:T(8,128)(2,1)}, u32[]{:S(2)}) copy-start(bf16[256,1024]{1,0:T(8,128)(2,1)} %refs_1_.1) | copy-start | bytes 1572868

commit v3 on v2

--- a/solution.py
+++ b/solution.py
@@ -3,7 +3,7 @@
 from jax import lax
 from jax.experimental import pallas as pl
 from jax.experimental.pallas import tpu as pltpu
-from jax.sharding import PartitionSpec as P
+from jax.sharding import Mesh, PartitionSpec as P
 
 HEAD_TOTAL = 8
 HEAD_DEPTH = 32
@@ -209,43 +209,46 @@
     pair_ref, proj_ref, msa_ref, chain_ref, chain_bias_ref, mask_ref = near
     queries, keys, width = pair_ref.shape
     cells = HEAD_TOTAL * queries
-    dap, seq = lax.axis_index("dap"), lax.axis_index("seq")
-    odd = lax.rem(dap, 2)
+    far, seq = lax.axis_index("far"), lax.axis_index("seq")
+    dap = far * lax.axis_size("near") + lax.axis_index("near")
     pairs = queries * keys
-    normed = normalize([pair_ref[...].astype(F32).reshape(pairs, width)], width)[0]
-    bias = lax.dot_general(
-        proj_ref[...], normed, (((1,), (1,)), ((), ())),
-        precision=lax.Precision.HIGHEST, preferred_element_type=F32,
-    )
+
+    block = jnp.concatenate(halves(msa_ref[0].astype(F32)), axis=0).astype(BF16)
+    out_ref[:, : block.shape[0], :] = jnp.broadcast_to(block[None], (out_ref.shape[0], *block.shape))
+
+    pair = pair_ref[...].astype(F32).reshape(pairs, width)
+    center = pair - jnp.sum(pair, axis=-1, keepdims=True) * (1.0 / width)
+    spread = jnp.sum(center * center, axis=-1, keepdims=True) * (1.0 / width)
+    shape = (pairs, LANES)
+    lane = iota(shape, 1)
+    bias = jnp.zeros(shape, F32)
+    for h in range(HEAD_TOTAL):
+        projected = jnp.sum(center * proj_ref[h : h + 1, :], axis=-1, keepdims=True)
+        bias = jnp.where(lane % cells // queries == h, projected, bias)
+    bias = bias * lax.rsqrt(spread + epsilon)
+    bias = jnp.where(lane % queries == iota(shape, 0) // keys, bias, 0.0)
+    bias = jnp.sum(bias.reshape(pairs // SUBLANES, SUBLANES, LANES), axis=0)
+    bias = bias + pltpu.roll(bias, keys, 0)
+
     shape = bias.shape
-    head, pair = iota(shape, 0), iota(shape, 1)
+    row, lane = iota(shape, 0), iota(shape, 1)
     key_chain, query_chain = jnp.zeros(shape, jnp.int32), jnp.zeros(shape, jnp.int32)
     for k in range(keys):
-        key_chain = jnp.where(pair % keys == k, chain_ref[dap * keys + k], key_chain)
+        key_chain = jnp.where(row % keys == k, chain_ref[dap * keys + k], key_chain)
     for k in range(queries):
-        query_chain = jnp.where(pair // keys == k, chain_ref[seq * queries + k], query_chain)
+        query_chain = jnp.where(lane % queries == k, chain_ref[seq * queries + k], query_chain)
     same, other = jnp.zeros(shape, F32), jnp.zeros(shape, F32)
     for h in range(HEAD_TOTAL):
-        same = jnp.where(head == h, chain_bias_ref[0, h], same)
-        other = jnp.where(head == h, chain_bias_ref[1, h], other)
-    bias = (bias + jnp.where(key_chain == query_chain, same, other)).astype(BF16)
-    heads = (iota((HEAD_TOTAL, LANES), 1) % cells // queries == iota((HEAD_TOTAL, LANES), 0)).astype(F32)
-    bias = lax.dot_general(
-        bias, heads.astype(BF16), (((0,), (0,)), ((), ())), preferred_element_type=F32
-    )
-    own = iota(bias.shape, 1) % queries == iota(bias.shape, 0) // keys
-    bias = jnp.where(own, bias, 0.0).reshape(pairs // SUBLANES, SUBLANES, LANES)
-    bias = jnp.sum(bias, axis=0)
-    bias = bias + pltpu.roll(bias, keys, 0)
-    shape = bias.shape
-    row, lane = iota(shape, 0), iota(shape, 1)
+        here = lane % cells // queries == h
+        same = jnp.where(here, chain_bias_ref[0, h], same)
+        other = jnp.where(here, chain_bias_ref[1, h], other)
     mask = jnp.zeros(shape, F32)
     for k in range(SUBLANES):
         mask = jnp.where(row == k, mask_ref[0, k].astype(F32), mask)
+    bias = bias + jnp.where(key_chain == query_chain, same, other)
     upper = (lane >= cells).astype(jnp.int32)
-    tail = jnp.where(upper != odd, bias, mask)
-    block = jnp.concatenate([*halves(msa_ref[0].astype(F32)), tail], axis=0).astype(BF16)
-    out_ref[...] = jnp.broadcast_to(block[None], out_ref.shape)
+    tail = jnp.where(upper != far, bias, mask).astype(BF16)
+    out_ref[:, block.shape[0] :, :] = jnp.broadcast_to(tail[None], (out_ref.shape[0], *tail.shape))
 
 
 def block_kernel(
@@ -264,26 +267,31 @@
     pl.semaphore_signal(fence, 1)
     pl.semaphore_wait(fence, 1)
     count, rows, _ = block_ref.shape
+    far_count, near_count = 2, count // seq_count // 2
     own_rows = SUBLANES
     width = rows * LANES // own_rows - LANES
     parts = width // LANES
-    members = count // seq_count
+    members = far_count * near_count
     residues = seq_count * own_rows
     heads, depth = HEAD_TOTAL, HEAD_DEPTH
     inner = heads * depth
     cells = heads * own_rows
     tokens = members * own_rows
-    dap, seq = lax.axis_index("dap"), lax.axis_index("seq")
+    seq = lax.axis_index("seq")
+    me = lax.axis_index("near") * far_count + lax.axis_index("far")
     scaling = depth**-0.5
 
     def part(ref_index, k):
         return block_ref[ref_index, k * own_rows : (k + 1) * own_rows, :].astype(F32)
 
+    def at(m, s):
+        return (m // far_count * seq_count + s) * far_count + m % far_count
+
     def tail(m, s):
-        return block_ref[m * seq_count + s, parts * own_rows :, :].astype(F32)
+        return block_ref[at(m, s), parts * own_rows :, :].astype(F32)
 
     def mine(k):
-        return jnp.concatenate([part(m * seq_count + seq, k) for m in range(members)], axis=0)
+        return jnp.concatenate([part(at(m, seq), k) for m in range(members)], axis=0)
 
     residual = [mine(k) for k in range(parts)]
     own = jnp.concatenate(normalize(residual, width), axis=1).astype(BF16)
@@ -304,10 +312,14 @@
     row, lane = iota(shape, 0), iota(shape, 1)
     lower = lane < cells
     bias = []
+    first = row < own_rows // 2
     for m in range(0, members, 2):
-        first = row < own_rows // 2
-        both = jnp.where(first, tail(m, seq), tail(m + 1, seq))
-        bias.append(jnp.where(first != lower, both, pltpu.roll(both, cells, 1)))
+        far = m // near_count
+        even, odd = (at((n - far * near_count) * far_count + far, seq) for n in (m, m + 1))
+        even, odd = (block_ref[n, parts * own_rows :, :].astype(F32) for n in (even, odd))
+        both = jnp.where(first, even, odd)
+        valid = lower if far else jnp.logical_not(lower)
+        bias.append(jnp.where(valid, both, pltpu.roll(both, cells, 1)))
     bias = jnp.concatenate(bias, axis=0)
     wide = iota((residues, LANES), 1) < cells
     keeps = [
@@ -316,6 +328,17 @@
         ) > 0
         for m in range(0, members, 2)
     ]
+
+    def unmix(two):
+        pieces = two.reshape(seq_count, far_count, own_rows, LANES)
+        return jnp.where(wide, pieces[:, 0].reshape(wide.shape), pieces[:, 1].reshape(wide.shape))
+
+    def remix(one):
+        pieces = [
+            half.reshape(seq_count, 1, own_rows, LANES)
+            for half in (jnp.where(wide, one, 0.0), jnp.where(wide, 0.0, one))
+        ]
+        return jnp.concatenate(pieces, axis=1).reshape(2 * residues, LANES)
 
     scores = [
         lax.dot_general(
@@ -326,14 +349,11 @@
         )
         for m in range(0, members, 2)
     ]
-    scores = [jnp.where(wide, two[:residues], two[residues:]) * scaling + bias for two in scores]
+    scores = [unmix(two) * scaling + bias for two in scores]
     scores = [jnp.where(keep, two, -1000000000.0) for two, keep in zip(scores, keeps)]
     scores = [jnp.exp(two - jnp.max(two, axis=0, keepdims=True)) for two in scores]
     weights = [two / jnp.sum(two, axis=0, keepdims=True) for two in scores]
-    weights = [
-        jnp.concatenate([jnp.where(wide, two, 0.0), jnp.where(wide, 0.0, two)], axis=0).astype(BF16)
-        for two in weights
-    ]
+    weights = [remix(two).astype(BF16) for two in weights]
     mixed = [
         lax.dot_general(
             two, all_values[2 * k * residues : 2 * (k + 1) * residues],
@@ -355,7 +375,7 @@
     second_ref[...] = second.reshape(members, own_rows, width)
     copies[1].wait()
     key_values = mm(second, column_proj_ref[:, inner : 3 * inner]).astype(BF16).astype(F32)
-    own = second_ref[dap]
+    own = second_ref[me]
     queries = mm(own, column_proj_ref[:, :inner]).astype(BF16).astype(F32)
     gates = mm(own, column_proj_ref[:, 3 * inner :]).astype(BF16).astype(F32)
     products = (
@@ -371,7 +391,7 @@
     keep = []
     for m in range(members):
         mask = tail(m, seq)
-        valid = lower if m % 2 == 0 else jnp.logical_not(lower)
+        valid = jnp.logical_not(lower) if m % far_count else lower
         mask = jnp.where(valid, mask, pltpu.roll(mask, cells, 1))
         keep.append(jnp.concatenate([mask] * (inner // LANES), axis=1)[None])
     keep = jnp.concatenate(keep, axis=0)
@@ -383,7 +403,7 @@
     )
     gated = (jax.nn.sigmoid(gates) * attended).astype(BF16)
     copies[2].wait()
-    two = one_ref[dap] + mm(gated, column_out_ref[...])
+    two = one_ref[me] + mm(gated, column_out_ref[...])
     copies[3].wait()
     hidden = jnp.maximum(mm(normalize_rows(two), expansion_ref[...]), 0.0).astype(BF16)
     copies[4].wait()
@@ -405,7 +425,8 @@
     contraction_matrix,
 ):
     _, own_rows, width = homolog_tensor.shape
-    dap_count, seq_count = lax.axis_size("dap"), lax.axis_size("seq")
+    seq_count = lax.axis_size("seq")
+    dap_count = lax.axis_size("far") * lax.axis_size("near")
     count = dap_count * seq_count
     rows = own_rows * (width // LANES + 1)
     vmem, hbm = (pl.BlockSpec(memory_space=space) for space in (pltpu.VMEM, pltpu.HBM))
@@ -423,7 +444,7 @@
         ],
         compiler_params=pltpu.CompilerParams(vmem_limit_bytes=8 << 20),
     )(*map(in_hbm, vectors + scalars))
-    blocks = lax.all_to_all(packed, ("dap", "seq"), split_axis=0, concat_axis=0, tiled=True)
+    blocks = lax.all_to_all(packed, ("near", "seq", "far"), split_axis=0, concat_axis=0, tiled=True)
     later = [
         horizontal_projector, column_proj, vertical_projector, expansion_matrix, contraction_matrix
     ]
@@ -447,43 +468,35 @@
     return pltpu.with_memory_space_constraint(operand, pltpu.HBM)
 
 
-def fits_whole(homolog_tensor, pair_features, dap_count):
-    row_count, local_residues, width = homolog_tensor.shape
-    queries, keys, pair_width = pair_features.shape
+def fits_whole(homolog_tensor, pair_features, dap_count, seq_count):
+    rows, residues, width = homolog_tensor.shape
+    _, _, pair_width = pair_features.shape
     return (
-        row_count == 1
-        and local_residues == SUBLANES
-        and queries == local_residues
-        and 2 * keys == SUBLANES
-        and dap_count % 2 == 0
-        and 2 * HEAD_TOTAL * queries == LANES
+        rows == dap_count
+        and residues == seq_count * SUBLANES
+        and 2 * residues == dap_count * SUBLANES
+        and dap_count % 4 == 0
+        and 2 * HEAD_TOTAL * SUBLANES == LANES
         and width % LANES == 0
         and pair_width == LANES
         and HEAD_TOTAL * HEAD_DEPTH % LANES == 0
-        and lax.axis_size("seq") * dap_count * homolog_tensor.size * 2 <= WHOLE_BYTES
-    )
-
-
-def choose(*operands):
-    whole = fits_whole(operands[0], operands[1], lax.axis_size("dap"))
-    return whole_body(*operands) if whole else body(*operands)
+        and homolog_tensor.size * 2 <= WHOLE_BYTES
+    )
 
 
 def solution(mesh):
-    placed = (
-        P("dap", "seq", None),
-        P("seq", "dap", None),
-        P("dap", "seq"),
-        P(),
-        P(),
-        P(),
-        P(),
-        P(),
-        P(),
-        P(),
-        P(),
-        P(),
-    )
-    return jax.shard_map(
-        choose, mesh=mesh, in_specs=placed, out_specs=P("dap", "seq", None), check_vma=False
-    )
+    def placed(dap):
+        return (P(dap, "seq", None), P("seq", dap, None), P(dap, "seq"), *[P()] * 9)
+
+    def step(*operands):
+        dap_count, seq_count = mesh.shape["dap"], mesh.shape["seq"]
+        if fits_whole(operands[0], operands[1], dap_count, seq_count):
+            devices = mesh.devices.reshape(2, dap_count // 2, seq_count)
+            used, chosen, dap = Mesh(devices, ("far", "near", "seq")), whole_body, ("far", "near")
+        else:
+            used, chosen, dap = mesh, body, "dap"
+        return jax.shard_map(
+            chosen, mesh=used, in_specs=placed(dap), out_specs=P(dap, "seq", None), check_vma=False
+        )(*operands)
+
+    return step

time: 20.9 us -> 19.6 us (0.938)
  blocking collectives: 16.4 us -> 15.4 us
  Pallas kernels: 4.33 us -> 4.04 us
    all_to_all x1, blocking collectives: 16.4 us -> 15.4 us  [whole_body(): lax.all_to_all(packed, ('near', 'seq', 'far'), split_axis=0, concat_axis=...]
    pallas_call x1, Pallas kernels: 1.39 us -> 1.1 us  [whole_body(): pl.pallas_call(pack_kernel, out_shape=jax.ShapeDtypeStruct((count, rows,...]
where the time goes in v3:
time: 19.6 us; the launch traced here: 19.4 us
  blocking collectives  15.4 us (79%)
  Pallas kernels  4.04 us (21%)
    all_to_all x1, blocking collectives, whole_body(): lax.all_to_all(packed, ('near', 'seq', 'far'), split_axis=0, concat_axis=...  15.4 us
    pallas_call x1, Pallas kernels, whole_body(): pl.pallas_call(lambda *refs: block_kernel(seq_count, *refs), out_shape=ja...  2.94 us
    pallas_call x1, Pallas kernels, whole_body(): pl.pallas_call(pack_kernel, out_shape=jax.ShapeDtypeStruct((count, rows,...  1.1 us

profile of v3, /device:TPU:0, one launch (start us, length us, event | category | flops | bytes accessed | tf_op | source)
XLA Modules:
  0.0 19.4 jit_solution(1679841186809528670)
XLA Ops:
  0.0 0.0 copy-start
  0.0 1.1 %shard_map.118 = bf16[32,24,128]{2,1,0:T(8,128)(2,1)S(1)} custom-call(bf16[8,4,128]{2,1,0:T(4,128)(2,1)} %refs_0_.1, f32[8,128]{1,0:T(8,128)} %bitcast.1, bf16[1,8,256]{2,1,0:T(8,128)(2,1)} %refs_2_.2, s32[32]{0:T(128)} %refs_3_.2, f32[2,8]{1,0:T(2,128)} %refs_4_.2, s32[1,8]{1,0:T(1,128)} %refs_5_.2), custom_call_target="tpu_custom_call" | custom-call | tf_op jit(solution)/shard_map/pallas_call | solution.py:435
  1.1 15.4 %all_to_all.5.refs_0_ = bf16[32,24,128]{2,1,0:T(8,128)(2,1)S(1)} all-to-all(bf16[32,24,128]{2,1,0:T(8,128)(2,1)S(1)} %shard_map.118), channel_id=1, replica_groups=mesh['far'=2,'near'=4,'seq'=4] {'near','seq','far'}, dimensions={0} | all-to-all | bytes 393216 | tf_op jit(solution)/shard_map/all_to_all | solution.py:447
  16.5 0.0 copy-done
  16.5 2.9 %shard_map.119 = bf16[1,8,256]{2,1,0:T(8,128)(2,1)} custom-call(bf16[32,24,128]{2,1,0:T(8,128)(2,1)S(1)} %all_to_all.5.refs_0_, bf16[256,1024]{1,0:T(8,128)(2,1)S(1)} %copy-done, bf16[256,256]{1,0:T(8,128)(2,1)} %refs_2_.3, bf16[256,1024]{1,0:T(8,128)(2,1)} %refs_3_.3, bf16[256,256]{1,0:T(8,128)(2,1)} %refs_4_.3, bf16[256,1024]{1,0:T(8,128)(2,1)} %refs_5_.3, ...), custom_call_target="tpu_custom_call" | custom-call | tf_op jit(solution)/shard_map/pallas_call | solution.py:451
Async XLA Ops:
  0.0 16.5 %copy-start = (bf16[256,1024]{1,0:T(8,128)(2,1)S(1)}, bf16[256,1024]{1,0:T(8,128)(2,1)}, u32[]{:S(2)}) copy-start(bf16[256,1024]{1,0:T(8,128)(2,1)} %refs_1_.1) | copy-start | bytes 1572868

commit v4 on v3

--- a/solution.py
+++ b/solution.py
@@ -1,3 +1,5 @@
+import functools
+
 import jax
 import jax.numpy as jnp
 from jax import lax
@@ -160,6 +162,7 @@
 
 LANES = 128
 SUBLANES = 8
+WAIT_FLOPS = 20_000_000_000
 WHOLE_BYTES = 1 << 20
 F32 = jnp.float32
 BF16 = jnp.bfloat16
@@ -252,20 +255,9 @@
 
 
 def block_kernel(
-    seq_count, block_ref, row_proj_ref, row_out_far, column_proj_far, column_out_far, expansion_far,
-    contraction_far, out_ref, second_ref, one_ref, row_out_ref, column_proj_ref,
-    column_out_ref, expansion_ref, contraction_ref, arrived, fence,
+    seq_count, block_ref, row_proj_ref, row_out_ref, column_proj_ref, column_out_ref, expansion_ref,
+    contraction_ref, out_ref, normed_ref, second_ref, one_ref,
 ):
-    far = (row_out_far, column_proj_far, column_out_far, expansion_far, contraction_far)
-    near = (row_out_ref, column_proj_ref, column_out_ref, expansion_ref, contraction_ref)
-    copies = [
-        pltpu.make_async_copy(source, target, arrived.at[k])
-        for k, (source, target) in enumerate(zip(far, near))
-    ]
-    for copy in copies:
-        copy.start()
-    pl.semaphore_signal(fence, 1)
-    pl.semaphore_wait(fence, 1)
     count, rows, _ = block_ref.shape
     far_count, near_count = 2, count // seq_count // 2
     own_rows = SUBLANES
@@ -294,12 +286,13 @@
         return jnp.concatenate([part(at(m, seq), k) for m in range(members)], axis=0)
 
     residual = [mine(k) for k in range(parts)]
-    own = jnp.concatenate(normalize(residual, width), axis=1).astype(BF16)
-    queries = mm(own, row_proj_ref[:, :inner]).astype(BF16).astype(F32)
-    gates = mm(own, row_proj_ref[:, 3 * inner :]).astype(BF16).astype(F32)
     everything = slice(None)
     x = [part(everything, k).reshape(count * own_rows, LANES) for k in range(parts)]
     normed = jnp.concatenate(normalize(x, width), axis=1).astype(BF16)
+    normed_ref[...] = normed.reshape(near_count, seq_count, far_count * own_rows, width)
+    own = normed_ref[:, seq].reshape(tokens, width)
+    queries = mm(own, row_proj_ref[:, :inner]).astype(BF16).astype(F32)
+    gates = mm(own, row_proj_ref[:, 3 * inner :]).astype(BF16).astype(F32)
     all_keys = mm(normed, row_proj_ref[:, inner : 2 * inner]).astype(BF16)
     all_values = mm(normed, row_proj_ref[:, 2 * inner : 3 * inner]).astype(BF16)
 
@@ -352,7 +345,7 @@
     scores = [unmix(two) * scaling + bias for two in scores]
     scores = [jnp.where(keep, two, -1000000000.0) for two, keep in zip(scores, keeps)]
     scores = [jnp.exp(two - jnp.max(two, axis=0, keepdims=True)) for two in scores]
-    weights = [two / jnp.sum(two, axis=0, keepdims=True) for two in scores]
+    weights = [two * (1.0 / jnp.sum(two, axis=0, keepdims=True)) for two in scores]
     weights = [remix(two).astype(BF16) for two in weights]
     mixed = [
         lax.dot_general(
@@ -367,13 +360,11 @@
     ]
     attended = jnp.concatenate(mixed, axis=0).reshape(tokens, inner)
     gated = (jax.nn.sigmoid(gates) * attended).astype(BF16)
-    copies[0].wait()
     one = (jnp.concatenate(residual, axis=1) + mm(gated, row_out_ref[...])).astype(BF16).astype(F32)
     one_ref[...] = one.reshape(members, own_rows, width)
 
     second = normalize_rows(one)
     second_ref[...] = second.reshape(members, own_rows, width)
-    copies[1].wait()
     key_values = mm(second, column_proj_ref[:, inner : 3 * inner]).astype(BF16).astype(F32)
     own = second_ref[me]
     queries = mm(own, column_proj_ref[:, :inner]).astype(BF16).astype(F32)
@@ -397,16 +388,13 @@
     keep = jnp.concatenate(keep, axis=0)
     scores = jnp.where(keep > 0, scores, -1000000000.0)
     scores = jnp.exp(scores - jnp.max(scores, axis=0, keepdims=True))
-    weights = (scores / jnp.sum(scores, axis=0, keepdims=True)).astype(BF16).astype(F32)
+    weights = (scores * (1.0 / jnp.sum(scores, axis=0, keepdims=True))).astype(BF16).astype(F32)
     attended = jnp.sum(
         weights * key_values[:, inner:].reshape(members, own_rows, inner), axis=0
     )
     gated = (jax.nn.sigmoid(gates) * attended).astype(BF16)
-    copies[2].wait()
     two = one_ref[me] + mm(gated, column_out_ref[...])
-    copies[3].wait()
     hidden = jnp.maximum(mm(normalize_rows(two), expansion_ref[...]), 0.0).astype(BF16)
-    copies[4].wait()
     out_ref[0] = (two + mm(hidden, contraction_ref[...])).astype(BF16)
 
 
@@ -443,25 +431,29 @@
             pltpu.SemaphoreType.DMA((len(vectors + scalars),)),
         ],
         compiler_params=pltpu.CompilerParams(vmem_limit_bytes=8 << 20),
+        cost_estimate=pl.CostEstimate(flops=WAIT_FLOPS, bytes_accessed=count * rows * LANES * 2, transcendentals=0),
     )(*map(in_hbm, vectors + scalars))
     blocks = lax.all_to_all(packed, ("near", "seq", "far"), split_axis=0, concat_axis=0, tiled=True)
-    later = [
-        horizontal_projector, column_proj, vertical_projector, expansion_matrix, contraction_matrix
-    ]
     return pl.pallas_call(
-        lambda *refs: block_kernel(seq_count, *refs),
+        functools.partial(block_kernel, seq_count),
         out_shape=jax.ShapeDtypeStruct(homolog_tensor.shape, BF16),
-        in_specs=[vmem] * 2 + [hbm] * len(later),
+        in_specs=[vmem] * 7,
         out_specs=vmem,
         scratch_shapes=[
+            pltpu.VMEM((dap_count // 2, seq_count, 2 * own_rows, width), BF16),
             pltpu.VMEM((dap_count, own_rows, width), BF16),
             pltpu.VMEM((dap_count, own_rows, width), F32),
-            *(pltpu.VMEM(weight.shape, weight.dtype) for weight in later),
-            pltpu.SemaphoreType.DMA((len(later),)),
-            pltpu.SemaphoreType.REGULAR,
         ],
         compiler_params=pltpu.CompilerParams(vmem_limit_bytes=16 << 20),
-    )(blocks, horizontal_matrices, *map(in_hbm, later))
+    )(
+        blocks,
+        horizontal_matrices,
+        horizontal_projector,
+        column_proj,
+        vertical_projector,
+        expansion_matrix,
+        contraction_matrix,
+    )
 
 
 def in_hbm(operand):

time: 19.6 us -> 19.3 us (0.985)
  Pallas kernels: 4.04 us -> 3.71 us
    pallas_call x1, Pallas kernels: 2.94 us -> 2.55 us  [whole_body(): pl.pallas_call(functools.partial(block_kernel, seq_count), out_shape=jax....]
where the time goes in v4:
time: 19.3 us; the launch traced here: 19.2 us
  blocking collectives  15.4 us (80%)
  Pallas kernels  3.71 us (19%)
    all_to_all x1, blocking collectives, whole_body(): lax.all_to_all(packed, ('near', 'seq', 'far'), split_axis=0, concat_axis=...  15.4 us
    pallas_call x1, Pallas kernels, whole_body(): pl.pallas_call(functools.partial(block_kernel, seq_count), out_shape=jax....  2.55 us
    pallas_call x1, Pallas kernels, whole_body(): pl.pallas_call(pack_kernel, out_shape=jax.ShapeDtypeStruct((count, rows,...  1.16 us

profile of v4, /device:TPU:0, one launch (start us, length us, event | category | flops | bytes accessed | tf_op | source)
XLA Modules:
  0.0 19.2 jit_solution(4709056014665194222)
XLA Ops:
  0.0 0.0 copy-start
  0.0 0.0 copy-start.1
  0.0 0.0 copy-start.2
  0.0 0.0 copy-start.3
  0.0 1.2 %shard_map.118 = bf16[32,24,128]{2,1,0:T(8,128)(2,1)S(1)} custom-call(bf16[8,4,128]{2,1,0:T(4,128)(2,1)} %refs_0_.1, f32[8,128]{1,0:T(8,128)} %bitcast.1, bf16[1,8,256]{2,1,0:T(8,128)(2,1)} %refs_2_.1, s32[32]{0:T(128)} %refs_3_.1, f32[2,8]{1,0:T(2,128)} %refs_4_.1, s32[1,8]{1,0:T(1,128)} %refs_5_.1), custom_call_target="tpu_custom_call" | custom-call | flops 20000000000 | bytes 196608 | tf_op jit(solution)/shard_map/pallas_call | solution.py:423
  1.2 0.0 copy-start.4
  1.2 0.0 copy-start.5
  1.2 15.4 %all_to_all.5.block_ref = bf16[32,24,128]{2,1,0:T(8,128)(2,1)S(1)} all-to-all(bf16[32,24,128]{2,1,0:T(8,128)(2,1)S(1)} %shard_map.118), channel_id=1, replica_groups=mesh['far'=2,'near'=4,'seq'=4] {'near','seq','far'}, dimensions={0} | all-to-all | bytes 393216 | tf_op jit(solution)/shard_map/all_to_all | solution.py:436
  16.6 0.0 copy-done
  16.6 0.0 copy-done.1
  16.6 0.0 copy-done.2
  16.6 0.0 copy-done.3
  16.6 0.0 copy-done.4
  16.6 0.0 copy-done.5
  16.6 2.5 %shard_map.119 = bf16[1,8,256]{2,1,0:T(8,128)(2,1)} custom-call(bf16[32,24,128]{2,1,0:T(8,128)(2,1)S(1)} %all_to_all.5.block_ref, bf16[256,1024]{1,0:T(8,128)(2,1)S(1)} %copy-done, bf16[256,256]{1,0:T(8,128)(2,1)S(1)} %copy-done.4, bf16[256,1024]{1,0:T(8,128)(2,1)S(1)} %copy-done.1, bf16[256,256]{1,0:T(8,128)(2,1)S(1)} %copy-done.5, ...), custom_call_target="tpu_custom_call" | custom-call | tf_op jit(solution)/shard_map/pallas_call | solution.py:437
Async XLA Ops:
  0.0 16.6 %copy-start = (bf16[256,1024]{1,0:T(8,128)(2,1)S(1)}, bf16[256,1024]{1,0:T(8,128)(2,1)}, u32[]{:S(2)}) copy-start(bf16[256,1024]{1,0:T(8,128)(2,1)} %row_proj_ref.1) | copy-start | bytes 1572868
  0.0 16.6 %copy-start.1 = (bf16[256,1024]{1,0:T(8,128)(2,1)S(1)}, bf16[256,1024]{1,0:T(8,128)(2,1)}, u32[]{:S(2)}) copy-start(bf16[256,1024]{1,0:T(8,128)(2,1)} %column_proj_ref.1) | copy-start | bytes 1572868
  0.0 16.6 %copy-start.2 = (bf16[256,1024]{1,0:T(8,128)(2,1)S(1)}, bf16[256,1024]{1,0:T(8,128)(2,1)}, u32[]{:S(2)}) copy-start(bf16[256,1024]{1,0:T(8,128)(2,1)} %expansion_ref.1) | copy-start | bytes 1572868
  0.0 16.6 %copy-start.3 = (bf16[1024,256]{1,0:T(8,128)(2,1)S(1)}, bf16[1024,256]{1,0:T(8,128)(2,1)}, u32[]{:S(2)}) copy-start(bf16[1024,256]{1,0:T(8,128)(2,1)} %contraction_ref.1) | copy-start | bytes 1572868
  1.2 15.4 %copy-start.4 = (bf16[256,256]{1,0:T(8,128)(2,1)S(1)}, bf16[256,256]{1,0:T(8,128)(2,1)}, u32[]{:S(2)}) copy-start(bf16[256,256]{1,0:T(8,128)(2,1)} %row_out_ref.1) | copy-start | bytes 393220
  1.2 15.4 %copy-start.5 = (bf16[256,256]{1,0:T(8,128)(2,1)S(1)}, bf16[256,256]{1,0:T(8,128)(2,1)}, u32[]{:S(2)}) copy-start(bf16[256,256]{1,0:T(8,128)(2,1)} %column_out_ref.1) | copy-start | bytes 393220

commit v5 on v4

--- a/solution.py
+++ b/solution.py
@@ -216,8 +216,12 @@
     dap = far * lax.axis_size("near") + lax.axis_index("near")
     pairs = queries * keys
 
-    block = jnp.concatenate(halves(msa_ref[0].astype(F32)), axis=0).astype(BF16)
-    out_ref[:, : block.shape[0], :] = jnp.broadcast_to(block[None], (out_ref.shape[0], *block.shape))
+    def spread_out(k, piece):
+        out_ref[:, k] = jnp.broadcast_to(piece.astype(BF16)[None], (out_ref.shape[0], *piece.shape))
+
+    block = jnp.concatenate(halves(msa_ref[0].astype(F32)), axis=0)
+    for k in range(block.shape[0] // keys):
+        spread_out(k, block[k * keys : (k + 1) * keys])
 
     pair = pair_ref[...].astype(F32).reshape(pairs, width)
     center = pair - jnp.sum(pair, axis=-1, keepdims=True) * (1.0 / width)
@@ -249,19 +253,18 @@
     for k in range(SUBLANES):
         mask = jnp.where(row == k, mask_ref[0, k].astype(F32), mask)
     bias = bias + jnp.where(key_chain == query_chain, same, other)
-    upper = (lane >= cells).astype(jnp.int32)
-    tail = jnp.where(upper != far, bias, mask).astype(BF16)
-    out_ref[:, block.shape[0] :, :] = jnp.broadcast_to(tail[None], (out_ref.shape[0], *tail.shape))
+    mask = jnp.where(lane == 0, mask, jnp.where(lane == 1, pltpu.roll(mask, keys, 0), 0.0))
+    spread_out(block.shape[0] // keys, jnp.where(lane >= cells, bias, mask)[:keys])
 
 
 def block_kernel(
     seq_count, block_ref, row_proj_ref, row_out_ref, column_proj_ref, column_out_ref, expansion_ref,
     contraction_ref, out_ref, normed_ref, second_ref, one_ref,
 ):
-    count, rows, _ = block_ref.shape
+    count, pieces, rows, _ = block_ref.shape
     far_count, near_count = 2, count // seq_count // 2
     own_rows = SUBLANES
-    width = rows * LANES // own_rows - LANES
+    width = (pieces - 1) * rows * LANES // own_rows
     parts = width // LANES
     members = far_count * near_count
     residues = seq_count * own_rows
@@ -274,13 +277,11 @@
     scaling = depth**-0.5
 
     def part(ref_index, k):
-        return block_ref[ref_index, k * own_rows : (k + 1) * own_rows, :].astype(F32)
+        halves_of = [block_ref[ref_index, 2 * k + n].astype(F32) for n in range(2)]
+        return jnp.concatenate(halves_of, axis=-2)
 
     def at(m, s):
         return (m // far_count * seq_count + s) * far_count + m % far_count
-
-    def tail(m, s):
-        return block_ref[at(m, s), parts * own_rows :, :].astype(F32)
 
     def mine(k):
         return jnp.concatenate([part(at(m, seq), k) for m in range(members)], axis=0)
@@ -305,19 +306,23 @@
     row, lane = iota(shape, 0), iota(shape, 1)
     lower = lane < cells
     bias = []
-    first = row < own_rows // 2
+    tails = block_ref[:, pieces - 1].astype(F32).reshape(count * rows, LANES).astype(BF16)
+    taken = iota((LANES, 2 * LANES), 0) == iota((LANES, 2 * LANES), 1) // LANES
+    masks = mm(tails, taken.astype(F32).astype(BF16))
+    masks = [half.reshape(count, rows, LANES) for half in halves(masks)]
+    masks = jnp.concatenate(masks, axis=1)
     for m in range(0, members, 2):
         far = m // near_count
         even, odd = (at((n - far * near_count) * far_count + far, seq) for n in (m, m + 1))
-        even, odd = (block_ref[n, parts * own_rows :, :].astype(F32) for n in (even, odd))
-        both = jnp.where(first, even, odd)
-        valid = lower if far else jnp.logical_not(lower)
-        bias.append(jnp.where(valid, both, pltpu.roll(both, cells, 1)))
+        both = [block_ref[n, pieces - 1].astype(F32) for n in (even, odd)]
+        both = jnp.concatenate(both, axis=0)
+        bias.append(jnp.where(lower, pltpu.roll(both, cells, 1), both))
     bias = jnp.concatenate(bias, axis=0)
     wide = iota((residues, LANES), 1) < cells
     keeps = [
         jnp.concatenate(
-            [jnp.where(lower, tail(m, s), tail(m + 1, s)) for s in range(seq_count)], axis=0
+            [jnp.where(lower, masks[at(m, s)], masks[at(m + 1, s)]) for s in range(seq_count)],
+            axis=0,
         ) > 0
         for m in range(0, members, 2)
     ]
@@ -381,9 +386,9 @@
     scores = scores.reshape(members, own_rows, inner)
     keep = []
     for m in range(members):
-        mask = tail(m, seq)
-        valid = jnp.logical_not(lower) if m % far_count else lower
-        mask = jnp.where(valid, mask, pltpu.roll(mask, cells, 1))
+        mask = masks[at(m, 0)]
+        for s in range(1, seq_count):
+            mask = jnp.where(seq == s, masks[at(m, s)], mask)
         keep.append(jnp.concatenate([mask] * (inner // LANES), axis=1)[None])
     keep = jnp.concatenate(keep, axis=0)
     scores = jnp.where(keep > 0, scores, -1000000000.0)
@@ -416,13 +421,14 @@
     seq_count = lax.axis_size("seq")
     dap_count = lax.axis_size("far") * lax.axis_size("near")
     count = dap_count * seq_count
-    rows = own_rows * (width // LANES + 1)
+    rows = own_rows // 2
+    pieces = 2 * width // LANES + 1
     vmem, hbm = (pl.BlockSpec(memory_space=space) for space in (pltpu.VMEM, pltpu.HBM))
     vectors = [pair_features, bias_proj.T, homolog_tensor]
     scalars = [chain_ids, chain_bias, entry_real_mask]
     packed = pl.pallas_call(
         pack_kernel,
-        out_shape=jax.ShapeDtypeStruct((count, rows, LANES), BF16),
+        out_shape=jax.ShapeDtypeStruct((count, pieces, rows, LANES), BF16),
         in_specs=[hbm] * len(vectors + scalars),
         out_specs=vmem,
         scratch_shapes=[
@@ -431,7 +437,7 @@
             pltpu.SemaphoreType.DMA((len(vectors + scalars),)),
         ],
         compiler_params=pltpu.CompilerParams(vmem_limit_bytes=8 << 20),
-        cost_estimate=pl.CostEstimate(flops=WAIT_FLOPS, bytes_accessed=count * rows * LANES * 2, transcendentals=0),
+        cost_estimate=pl.CostEstimate(flops=WAIT_FLOPS, bytes_accessed=count * pieces * rows * LANES * 2, transcendentals=0),
     )(*map(in_hbm, vectors + scalars))
     blocks = lax.all_to_all(packed, ("near", "seq", "far"), split_axis=0, concat_axis=0, tiled=True)
     return pl.pallas_call(

time: 19.3 us -> 19.1 us (0.990)
  blocking collectives: 15.4 us -> 15.1 us
    all_to_all x1, blocking collectives: 15.4 us -> 15.1 us  [whole_body(): lax.all_to_all(packed, ('near', 'seq', 'far'), split_axis=0, concat_axis=...]
where the time goes in v5:
time: 19.1 us; the launch traced here: 18.9 us
  blocking collectives  15.1 us (79%)
  Pallas kernels  3.72 us (19%)
    all_to_all x1, blocking collectives, whole_body(): lax.all_to_all(packed, ('near', 'seq', 'far'), split_axis=0, concat_axis=...  15.1 us
    pallas_call x1, Pallas kernels, whole_body(): pl.pallas_call(functools.partial(block_kernel, seq_count), out_shape=jax....  2.56 us
    pallas_call x1, Pallas kernels, whole_body(): pl.pallas_call(pack_kernel, out_shape=jax.ShapeDtypeStruct((count, pieces...  1.16 us

profile of v5, /device:TPU:0, one launch (start us, length us, event | category | flops | bytes accessed | tf_op | source)
XLA Modules:
  0.0 18.9 jit_solution(2506459458105690751)
XLA Ops:
  0.0 0.0 copy-start
  0.0 0.0 copy-start.1
  0.0 0.0 copy-start.2
  0.0 0.0 copy-start.3
  0.0 1.2 %shard_map.118 = bf16[32,5,4,128]{3,2,1,0:T(4,128)(2,1)S(1)} custom-call(bf16[8,4,128]{2,1,0:T(4,128)(2,1)} %refs_0_.1, f32[8,128]{1,0:T(8,128)} %bitcast.1, bf16[1,8,256]{2,1,0:T(8,128)(2,1)} %refs_2_.1, s32[32]{0:T(128)} %refs_3_.1, f32[2,8]{1,0:T(2,128)} %refs_4_.1, s32[1,8]{1,0:T(1,128)} %refs_5_.1), custom_call_target="tpu_custom_call" | custom-call | flops 20000000000 | bytes 163840 | tf_op jit(solution)/shard_map/pallas_call | solution.py:429
  1.2 0.0 copy-start.4
  1.2 0.0 copy-start.5
  1.2 15.1 %all_to_all.5.block_ref = bf16[32,5,4,128]{3,2,1,0:T(4,128)(2,1)S(1)} all-to-all(bf16[32,5,4,128]{3,2,1,0:T(4,128)(2,1)S(1)} %shard_map.118), channel_id=1, replica_groups=mesh['far'=2,'near'=4,'seq'=4] {'near','seq','far'}, dimensions={0} | all-to-all | bytes 327680 | tf_op jit(solution)/shard_map/all_to_all | solution.py:442
  16.3 0.0 copy-done
  16.3 0.0 copy-done.1
  16.3 0.0 copy-done.2
  16.4 0.0 copy-done.3
  16.4 0.0 copy-done.4
  16.4 0.0 copy-done.5
  16.4 2.6 %shard_map.119 = bf16[1,8,256]{2,1,0:T(8,128)(2,1)} custom-call(bf16[32,5,4,128]{3,2,1,0:T(4,128)(2,1)S(1)} %all_to_all.5.block_ref, bf16[256,1024]{1,0:T(8,128)(2,1)S(1)} %copy-done, bf16[256,256]{1,0:T(8,128)(2,1)S(1)} %copy-done.4, bf16[256,1024]{1,0:T(8,128)(2,1)S(1)} %copy-done.1, bf16[256,256]{1,0:T(8,128)(2,1)S(1)} %copy-done.5, ...), custom_call_target="tpu_custom_call" | custom-call | tf_op jit(solution)/shard_map/pallas_call | solution.py:443
Async XLA Ops:
  0.0 16.3 %copy-start = (bf16[256,1024]{1,0:T(8,128)(2,1)S(1)}, bf16[256,1024]{1,0:T(8,128)(2,1)}, u32[]{:S(2)}) copy-start(bf16[256,1024]{1,0:T(8,128)(2,1)} %row_proj_ref.1) | copy-start | bytes 1572868
  0.0 16.3 %copy-start.1 = (bf16[256,1024]{1,0:T(8,128)(2,1)S(1)}, bf16[256,1024]{1,0:T(8,128)(2,1)}, u32[]{:S(2)}) copy-start(bf16[256,1024]{1,0:T(8,128)(2,1)} %column_proj_ref.1) | copy-start | bytes 1572868
  0.0 16.3 %copy-start.2 = (bf16[256,1024]{1,0:T(8,128)(2,1)S(1)}, bf16[256,1024]{1,0:T(8,128)(2,1)}, u32[]{:S(2)}) copy-start(bf16[256,1024]{1,0:T(8,128)(2,1)} %expansion_ref.1) | copy-start | bytes 1572868
  0.0 16.3 %copy-start.3 = (bf16[1024,256]{1,0:T(8,128)(2,1)S(1)}, bf16[1024,256]{1,0:T(8,128)(2,1)}, u32[]{:S(2)}) copy-start(bf16[1024,256]{1,0:T(8,128)(2,1)} %contraction_ref.1) | copy-start | bytes 1572868
  1.2 15.2 %copy-start.4 = (bf16[256,256]{1,0:T(8,128)(2,1)S(1)}, bf16[256,256]{1,0:T(8,128)(2,1)}, u32[]{:S(2)}) copy-start(bf16[256,256]{1,0:T(8,128)(2,1)} %row_out_ref.1) | copy-start | bytes 393220
  1.2 15.2 %copy-start.5 = (bf16[256,256]{1,0:T(8,128)(2,1)S(1)}, bf16[256,256]{1,0:T(8,128)(2,1)}, u32[]{:S(2)}) copy-start(bf16[256,256]{1,0:T(8,128)(2,1)} %column_out_ref.1) | copy-start | bytes 393220

commit v6 on v5

--- a/solution.py
+++ b/solution.py
@@ -220,8 +220,9 @@
         out_ref[:, k] = jnp.broadcast_to(piece.astype(BF16)[None], (out_ref.shape[0], *piece.shape))
 
     block = jnp.concatenate(halves(msa_ref[0].astype(F32)), axis=0)
-    for k in range(block.shape[0] // keys):
-        spread_out(k, block[k * keys : (k + 1) * keys])
+    last = block.shape[0] // keys
+    for k in range(last):
+        spread_out(far + k, block[k * keys : (k + 1) * keys])
 
     pair = pair_ref[...].astype(F32).reshape(pairs, width)
     center = pair - jnp.sum(pair, axis=-1, keepdims=True) * (1.0 / width)
@@ -254,18 +255,18 @@
         mask = jnp.where(row == k, mask_ref[0, k].astype(F32), mask)
     bias = bias + jnp.where(key_chain == query_chain, same, other)
     mask = jnp.where(lane == 0, mask, jnp.where(lane == 1, pltpu.roll(mask, keys, 0), 0.0))
-    spread_out(block.shape[0] // keys, jnp.where(lane >= cells, bias, mask)[:keys])
+    spread_out((1 - far) * last, jnp.where(lane >= cells, bias, mask)[:keys])
 
 
 def block_kernel(
     seq_count, block_ref, row_proj_ref, row_out_ref, column_proj_ref, column_out_ref, expansion_ref,
     contraction_ref, out_ref, normed_ref, second_ref, one_ref,
 ):
-    count, pieces, rows, _ = block_ref.shape
-    far_count, near_count = 2, count // seq_count // 2
-    own_rows = SUBLANES
-    width = (pieces - 1) * rows * LANES // own_rows
-    parts = width // LANES
+    couples, pieces, own_rows, _ = block_ref.shape
+    far_count, near_count = 2, couples // seq_count
+    count = far_count * couples
+    parts = (pieces - 1) // far_count
+    width = parts * LANES
     members = far_count * near_count
     residues = seq_count * own_rows
     heads, depth = HEAD_TOTAL, HEAD_DEPTH
@@ -276,19 +277,22 @@
     me = lax.axis_index("near") * far_count + lax.axis_index("far")
     scaling = depth**-0.5
 
-    def part(ref_index, k):
-        halves_of = [block_ref[ref_index, 2 * k + n].astype(F32) for n in range(2)]
-        return jnp.concatenate(halves_of, axis=-2)
-
-    def at(m, s):
-        return (m // far_count * seq_count + s) * far_count + m % far_count
+    def part(couple, far, k):
+        return block_ref[couple, far * (parts + 1) + k].astype(F32)
+
+    def tail(near, s):
+        return block_ref[near * seq_count + s, parts].astype(F32)
 
     def mine(k):
-        return jnp.concatenate([part(at(m, seq), k) for m in range(members)], axis=0)
+        couple = [near * seq_count + seq for near in range(near_count)]
+        return jnp.concatenate([part(n, far, k) for n in couple for far in range(far_count)], axis=0)
+
+    def whole(k):
+        both = [part(slice(None), far, k)[:, None] for far in range(far_count)]
+        return jnp.concatenate(both, axis=1).reshape(count * own_rows, LANES)
 
     residual = [mine(k) for k in range(parts)]
-    everything = slice(None)
-    x = [part(everything, k).reshape(count * own_rows, LANES) for k in range(parts)]
+    x = [whole(k) for k in range(parts)]
     normed = jnp.concatenate(normalize(x, width), axis=1).astype(BF16)
     normed_ref[...] = normed.reshape(near_count, seq_count, far_count * own_rows, width)
     own = normed_ref[:, seq].reshape(tokens, width)
@@ -306,25 +310,30 @@
     row, lane = iota(shape, 0), iota(shape, 1)
     lower = lane < cells
     bias = []
-    tails = block_ref[:, pieces - 1].astype(F32).reshape(count * rows, LANES).astype(BF16)
-    taken = iota((LANES, 2 * LANES), 0) == iota((LANES, 2 * LANES), 1) // LANES
-    masks = mm(tails, taken.astype(F32).astype(BF16))
-    masks = [half.reshape(count, rows, LANES) for half in halves(masks)]
-    masks = jnp.concatenate(masks, axis=1)
-    for m in range(0, members, 2):
-        far = m // near_count
-        even, odd = (at((n - far * near_count) * far_count + far, seq) for n in (m, m + 1))
-        both = [block_ref[n, pieces - 1].astype(F32) for n in (even, odd)]
-        both = jnp.concatenate(both, axis=0)
-        bias.append(jnp.where(lower, pltpu.roll(both, cells, 1), both))
+    first = row < own_rows // 2
+
+    def swap(x):
+        return pltpu.roll(x, own_rows // 2, 0)
+
+    for far in range(far_count):
+        for near in range(0, near_count, 2):
+            even, odd = tail(near, seq), tail(near + 1, seq)
+            both = jnp.where(first, swap(even), odd) if far else jnp.where(first, even, swap(odd))
+            bias.append(jnp.where(lower, pltpu.roll(both, cells, 1), both))
     bias = jnp.concatenate(bias, axis=0)
     wide = iota((residues, LANES), 1) < cells
+    taken = iota((LANES, 2 * LANES), 0) == iota((LANES, 2 * LANES), 1) // LANES
+    masks = mm(block_ref[:, parts].reshape(couples * own_rows, LANES), taken.astype(F32).astype(BF16))
+    masks = [half.reshape(couples, own_rows, LANES) for half in halves(masks)]
+    masks = [(masks[0][n], masks[1][n]) for n in range(couples)]
+    masks = [
+        (jnp.where(first, one, swap(two)), jnp.where(first, swap(one), two)) for one, two in masks
+    ]
     keeps = [
         jnp.concatenate(
-            [jnp.where(lower, masks[at(m, s)], masks[at(m + 1, s)]) for s in range(seq_count)],
-            axis=0,
+            [jnp.where(lower, *masks[near * seq_count + s]) for s in range(seq_count)], axis=0
         ) > 0
-        for m in range(0, members, 2)
+        for near in range(near_count)
     ]
 
     def unmix(two):
@@ -386,9 +395,10 @@
     scores = scores.reshape(members, own_rows, inner)
     keep = []
     for m in range(members):
-        mask = masks[at(m, 0)]
+        couple, far = m // far_count * seq_count, m % far_count
+        mask = masks[couple][far]
         for s in range(1, seq_count):
-            mask = jnp.where(seq == s, masks[at(m, s)], mask)
+            mask = jnp.where(seq == s, masks[couple + s][far], mask)
         keep.append(jnp.concatenate([mask] * (inner // LANES), axis=1)[None])
     keep = jnp.concatenate(keep, axis=0)
     scores = jnp.where(keep > 0, scores, -1000000000.0)
@@ -440,6 +450,7 @@
         cost_estimate=pl.CostEstimate(flops=WAIT_FLOPS, bytes_accessed=count * pieces * rows * LANES * 2, transcendentals=0),
     )(*map(in_hbm, vectors + scalars))
     blocks = lax.all_to_all(packed, ("near", "seq", "far"), split_axis=0, concat_axis=0, tiled=True)
+    blocks = blocks.reshape(count // 2, pieces, 2 * rows, LANES)
     return pl.pallas_call(
         functools.partial(block_kernel, seq_count),
         out_shape=jax.ShapeDtypeStruct(homolog_tensor.shape, BF16),

time: 19.1 us -> 19.1 us (level)
  no operation moved by 1% of the time
where the time goes in v6:
time: 19.1 us; the launch traced here: 18.9 us
  blocking collectives  15.1 us (79%)
  Pallas kernels  3.71 us (19%)
    all_to_all x1, blocking collectives, whole_body(): lax.all_to_all(packed, ('near', 'seq', 'far'), split_axis=0, concat_axis=...  15.1 us
    pallas_call x1, Pallas kernels, whole_body(): pl.pallas_call(functools.partial(block_kernel, seq_count), out_shape=jax....  2.55 us
    pallas_call x1, Pallas kernels, whole_body(): pl.pallas_call(pack_kernel, out_shape=jax.ShapeDtypeStruct((count, pieces...  1.16 us

profile of v6, /device:TPU:0, one launch (start us, length us, event | category | flops | bytes accessed | tf_op | source)
XLA Modules:
  0.0 18.9 jit_solution(16779675608515924347)
XLA Ops:
  0.0 0.0 copy-start
  0.0 0.0 copy-start.1
  0.0 0.0 copy-start.2
  0.0 0.0 copy-start.3
  0.0 1.2 %shard_map.118 = bf16[32,5,4,128]{3,2,1,0:T(4,128)(2,1)S(1)} custom-call(bf16[8,4,128]{2,1,0:T(4,128)(2,1)} %refs_0_.1, f32[8,128]{1,0:T(8,128)} %bitcast.3, bf16[1,8,256]{2,1,0:T(8,128)(2,1)} %refs_2_.1, s32[32]{0:T(128)} %refs_3_.1, f32[2,8]{1,0:T(2,128)} %refs_4_.1, s32[1,8]{1,0:T(1,128)} %refs_5_.1), custom_call_target="tpu_custom_call" | custom-call | flops 20000000000 | bytes 163840 | tf_op jit(solution)/shard_map/pallas_call | solution.py:439
  1.2 0.0 copy-start.4
  1.2 0.0 copy-start.5
  1.2 15.1 %all_to_all.5 = bf16[32,5,4,128]{3,2,1,0:T(4,128)(2,1)S(1)} all-to-all(bf16[32,5,4,128]{3,2,1,0:T(4,128)(2,1)S(1)} %shard_map.118), channel_id=1, replica_groups=mesh['far'=2,'near'=4,'seq'=4] {'near','seq','far'}, dimensions={0} | all-to-all | bytes 327680 | tf_op jit(solution)/shard_map/all_to_all | solution.py:452
  16.3 0.0 copy-done
  16.3 0.0 copy-done.1
  16.3 0.0 copy-done.2
  16.4 0.0 copy-done.3
  16.4 0.0 copy-done.4
  16.4 0.0 copy-done.5
  16.4 2.6 %shard_map.119 = bf16[1,8,256]{2,1,0:T(8,128)(2,1)} custom-call(bf16[16,5,8,128]{3,2,1,0:T(8,128)(2,1)S(1)} %bitcast.2, bf16[256,1024]{1,0:T(8,128)(2,1)S(1)} %copy-done, bf16[256,256]{1,0:T(8,128)(2,1)S(1)} %copy-done.4, bf16[256,1024]{1,0:T(8,128)(2,1)S(1)} %copy-done.1, bf16[256,256]{1,0:T(8,128)(2,1)S(1)} %copy-done.5, bf16[256,1024]{1,0:T(8,128)(2,1)S(1)} %copy-done.2, ...), custom_call_target="tpu_custom_call" | custom-call | tf_op jit(solution)/shard_map/pallas_call | solution.py:454
Async XLA Ops:
  0.0 16.3 %copy-start = (bf16[256,1024]{1,0:T(8,128)(2,1)S(1)}, bf16[256,1024]{1,0:T(8,128)(2,1)}, u32[]{:S(2)}) copy-start(bf16[256,1024]{1,0:T(8,128)(2,1)} %row_proj_ref.1) | copy-start | bytes 1572868
  0.0 16.3 %copy-start.1 = (bf16[256,1024]{1,0:T(8,128)(2,1)S(1)}, bf16[256,1024]{1,0:T(8,128)(2,1)}, u32[]{:S(2)}) copy-start(bf16[256,1024]{1,0:T(8,128)(2,1)} %column_proj_ref.1) | copy-start | bytes 1572868
  0.0 16.3 %copy-start.2 = (bf16[256,1024]{1,0:T(8,128)(2,1)S(1)}, bf16[256,1024]{1,0:T(8,128)(2,1)}, u32[]{:S(2)}) copy-start(bf16[256,1024]{1,0:T(8,128)(2,1)} %expansion_ref.1) | copy-start | bytes 1572868
  0.0 16.3 %copy-start.3 = (bf16[1024,256]{1,0:T(8,128)(2,1)S(1)}, bf16[1024,256]{1,0:T(8,128)(2,1)}, u32[]{:S(2)}) copy-start(bf16[1024,256]{1,0:T(8,128)(2,1)} %contraction_ref.1) | copy-start | bytes 1572868
  1.2 15.2 %copy-start.4 = (bf16[256,256]{1,0:T(8,128)(2,1)S(1)}, bf16[256,256]{1,0:T(8,128)(2,1)}, u32[]{:S(2)}) copy-start(bf16[256,256]{1,0:T(8,128)(2,1)} %row_out_ref.1) | copy-start | bytes 393220
  1.2 15.2 %copy-start.5 = (bf16[256,256]{1,0:T(8,128)(2,1)S(1)}, bf16[256,256]{1,0:T(8,128)(2,1)}, u32[]{:S(2)}) copy-start(bf16[256,256]{1,0:T(8,128)(2,1)} %column_out_ref.1) | copy-start | bytes 393220
